TPU v7x, 32 devices: a whole 2x2x4 slice. The times are simulated.
32 devices in a mesh: rep: 16 (over z, y, x), section: 2 (over core).
Axes of the slice: x: 2, y: 2, z: 4, core: 2. Of those that a mesh axis runs over, the one named last changes fastest.
Arguments:
- ends: bfloat16 [2, 16, 2, 128, 1024], P('section', 'rep'), may hold values from -6 to 6
- w_gate: bfloat16 [2, 16, 1024, 256], P('section', 'rep'), may hold values from -6 to 6
- w_up: bfloat16 [2, 16, 1024, 256], P('section', 'rep'), may hold values from -6 to 6
- slow_down: bfloat16 [2, 16, 256, 1024], P('section', 'rep'), may hold values from -6 to 6
- adam_m: bfloat16 [2, 16, 256, 1024], P('section', 'rep'), may hold values from -2 to 2
- adam_v: bfloat16 [2, 16, 256, 1024], P('section', 'rep'), may hold values from 0.019897461 to 0.19921875
- momentum: bfloat16 [2, 16, 256, 1024], P('section', 'rep'), may hold values from -6 to 6
- routes: int32 [2, 16], replicated, may hold values from 0 to 15, as said below
- partner: int32 [16], replicated, may hold values from 0 to 15, as said below
Outputs:
- new_slow: bfloat16 [2, 16, 256, 1024], P('section', 'rep')
- new_momentum: bfloat16 [2, 16, 256, 1024], P('section', 'rep')
Inputs may be any that keep to these rules, and one draw needn't show every extreme that they name: For each micro-batch b there is one number k_b with 1 <= k_b < 16, and routes[b, r] is r with the bits of k_b flipped (bitwise exclusive or). partner[r] is r with the bits of one number of 1 to 3 flipped, the same number for the four replicas of each aligned group of four, so partner[partner[r]] = r.
All inputs are finite; a program needn't handle non-finite values.
Results may differ from a plain program's by a relative error of at most 0.0036.
Values may be sent and summed in bfloat16 or wider, within the bound.
A program may use at most 64 MiB of HBM per device.

v0:
```python
import functools

import jax
import jax.numpy as jnp
from jax import lax
from jax.experimental import pallas as pl
from jax.experimental.pallas import tpu as pltpu
from jax.sharding import PartitionSpec as P


def partner_2(x, axis, bit):
    return lax.ppermute(x, axis, [(i, i ^ 1 << bit) for i in range(lax.axis_size(axis))])


def forward_rows(in_rows, w_gate, w_up, w_down):
    model_width = in_rows.shape[1]
    hidden_units = w_gate.shape[1]
    as_float = in_rows.astype(jnp.float32)
    row_scale = lax.rsqrt(jnp.mean(as_float * as_float, axis=1, keepdims=True) + 1e-06)
    normed = (as_float * row_scale).astype(jnp.bfloat16)
    gate_act = jnp.dot(normed, w_gate, preferred_element_type=jnp.float32) * model_width ** (-0.5)
    up_act = jnp.dot(normed, w_up, preferred_element_type=jnp.float32) * model_width ** (-0.5)
    hidden = (jax.nn.silu(gate_act) * up_act).astype(jnp.bfloat16)
    branch = jnp.dot(hidden, w_down, preferred_element_type=jnp.float32) * hidden_units ** (-0.5)
    result = (as_float + branch).astype(jnp.bfloat16)
    return (result, (row_scale, gate_act, up_act, hidden))


def contract_last(left, right):
    return lax.dot_general(
        left, right, (((1,), (1,)), ((), ())), preferred_element_type=jnp.float32
    )


def grad_rows(cotangent, hidden, hidden_units):
    return lax.dot_general(
        hidden, cotangent, (((0,), (0,)), ((), ())), preferred_element_type=jnp.float32
    ) * hidden_units ** (-0.5)


def backward_rows(cotangent, in_rows, saved_state, w_gate, w_up, w_down):
    row_scale, gate_act, up_act, hidden = saved_state
    model_width = in_rows.shape[1]
    hidden_units = w_gate.shape[1]
    d_hidden = contract_last(cotangent, w_down) * hidden_units ** (-0.5)
    grad_term = grad_rows(cotangent, hidden, hidden_units)
    sigmoid_gate = jax.nn.sigmoid(gate_act)
    d_gate = (d_hidden * up_act * sigmoid_gate * (1.0 + gate_act * (1.0 - sigmoid_gate))).astype(
        jnp.bfloat16
    )
    d_up = (d_hidden * gate_act * sigmoid_gate).astype(jnp.bfloat16)
    d_normed = (contract_last(d_gate, w_gate) + contract_last(d_up, w_up)) * model_width ** (-0.5)
    as_float = in_rows.astype(jnp.float32)
    back_rows = (
        cotangent.astype(jnp.float32)
        + row_scale * d_normed
        - as_float * row_scale**3 * jnp.mean(d_normed * as_float, axis=1, keepdims=True)
    )
    return (grad_term, back_rows.astype(jnp.bfloat16))


def send_rows(payload, flip_key, source):
    replicas = lax.axis_size("rep")
    bits = replicas.bit_length() - 1
    starts = list(range(0, bits, 4))
    for start in starts:
        width = min(4, bits - start)
        target = 1 - source if start == starts[-1] else source

        def branch(flip, start=start, target=target):
            pairs = [
                (2 * r + source, 2 * (r ^ flip << start) + target) for r in range(replicas)
            ]

            def run(rows):
                if target == source and flip == 0:
                    return rows
                return lax.ppermute(rows, ("rep", "section"), pairs)

            return run

        payload = lax.switch(
            flip_key >> start & (1 << width) - 1, [branch(f) for f in range(1 << width)], payload
        )
    return payload


def outer_kernel(
    chunks, masks, grad, first_in, second_in, slow, mate_slow, momentum,
    new_slow, new_momentum, own, near, chosen, far, send_near, recv_near, send_far, recv_far,
):
    me = lax.axis_index("rep")
    peers = (me + 1 - 2 * (me % 2), me + 2 - 4 * ((me // 2) % 2))
    rows = grad.shape[0] // chunks
    f32, bf16 = jnp.float32, jnp.bfloat16

    barrier = pltpu.get_barrier_semaphore()
    for peer in peers:
        pl.semaphore_signal(
            barrier, inc=1, device_id={"rep": peer}, device_id_type=pl.DeviceIdType.MESH
        )

    def part(c):
        return pl.ds(pl.multiple_of(c * rows, rows), rows)

    def near_copy(c):
        return pltpu.make_async_remote_copy(
            src_ref=own.at[part(c)], dst_ref=near.at[part(c)],
            send_sem=send_near.at[c], recv_sem=recv_near.at[c],
            device_id={"rep": peers[0]}, device_id_type=pl.DeviceIdType.MESH,
        )

    def far_copy(c):
        return pltpu.make_async_remote_copy(
            src_ref=chosen.at[part(c)], dst_ref=far.at[part(c)],
            send_sem=send_far.at[c], recv_sem=recv_far.at[c],
            device_id={"rep": peers[1]}, device_id_type=pl.DeviceIdType.MESH,
        )

    def adam(c):
        p = part(c)
        g = grad[p, :]
        first = 0.9 * first_in[p, :].astype(f32) + 0.1 * g
        second = 0.999 * second_in[p, :].astype(f32) + 0.001 * g * g
        step = first / (jnp.sqrt(second) + 1e-08)
        own[p, :] = (step + 0.1 * slow[p, :].astype(f32)).astype(bf16)

    adam(0)
    pl.semaphore_wait(barrier, 2)
    near_copy(0).start()

    def begin(c, carry):
        adam(c)
        near_copy(c).start()
        return carry

    lax.fori_loop(1, chunks, begin, 0)

    def pass_on(c):
        p = part(c)
        near_copy(c).wait_recv()
        chosen[p, :] = jnp.where(
            masks[0:1, :] == 1, near[p, :].astype(f32), own[p, :].astype(f32)
        ).astype(bf16)
        far_copy(c).start()

    def finish(c):
        p = part(c)
        far_copy(c).wait_recv()
        mate = jnp.where(masks[1:2, :] == 1, far[p, :].astype(f32), chosen[p, :].astype(f32))
        mean = 0.5 * (own[p, :].astype(f32) + mate)
        moment = 0.9 * momentum[p, :].astype(f32) + mean
        averaged = 0.5 * (slow[p, :].astype(f32) + mate_slow[p, :].astype(f32))
        new_slow[p, :] = (averaged - 0.014 * (0.9 * moment + mean)).astype(bf16)
        new_momentum[p, :] = moment.astype(bf16)

    lag = 2

    def steady(c, carry):
        pass_on(c)

        @pl.when(c >= lag)
        def _():
            finish(c - lag)

        return carry

    lax.fori_loop(0, chunks, steady, 0)

    def drain(c, carry):
        finish(c)
        return carry

    lax.fori_loop(chunks - lag, chunks, drain, 0)

    def settle(c, carry):
        near_copy(c).wait_send()
        far_copy(c).wait_send()
        return carry

    lax.fori_loop(0, chunks, settle, 0)


def outer_update(masks, grad, first_in, second_in, slow, mate_slow, momentum):
    hidden_units, model_width = grad.shape
    chunks = hidden_units // 16
    block = pltpu.VMEM((hidden_units, model_width), jnp.bfloat16)
    sems = pltpu.SemaphoreType.DMA((chunks,))
    out = jax.ShapeDtypeStruct((hidden_units, model_width), jnp.bfloat16)
    in_vmem = pl.BlockSpec(memory_space=pltpu.VMEM)
    return pl.pallas_call(
        functools.partial(outer_kernel, chunks),
        out_shape=(out, out),
        in_specs=[in_vmem] * 7,
        out_specs=(in_vmem, in_vmem),
        scratch_shapes=[block] * 4 + [sems] * 4,
        compiler_params=pltpu.CompilerParams(
            collective_id=0, has_side_effects=True, vmem_limit_bytes=16 * 1024 * 1024
        ),
        name="outer",
    )(masks, grad, first_in, second_in, slow, mate_slow, momentum)


def on_device(ends, w_gate, w_up, slow_down, adam_m, adam_v, momentum, routes, partner):
    micro_count, row_count, model_width = ends.shape[2:]
    own_data = ends.reshape(micro_count * row_count, model_width)
    gate_w = w_gate[0, 0]
    up_w = w_up[0, 0]
    down_w = slow_down[0, 0]
    hidden_units = gate_w.shape[1]
    replica = lax.axis_index("rep")
    on_first = lax.axis_index("section") == 0
    flip_keys = routes[:, 0]
    flip_bits = jnp.bitwise_xor(partner[replica], replica)
    near_slow = partner_2(down_w, "rep", 0)

    def cut(rows):
        return rows.reshape(micro_count, row_count, model_width)

    def first_forward():
        result, saved = forward_rows(own_data, gate_w, up_w, down_w)
        return result, saved[3]

    def first_idle():
        return own_data, jnp.zeros((own_data.shape[0], hidden_units), jnp.bfloat16)

    sent, hidden = lax.cond(on_first, first_forward, first_idle)
    sent = cut(sent)
    arrived = [send_rows(sent[b], flip_keys[b], 0) for b in range(micro_count)]
    near_slow, *arrived = lax.optimization_barrier((near_slow, *arrived))
    arrived = jnp.concatenate(arrived)
    chosen_slow = jnp.where(flip_bits & 1 == 1, near_slow, down_w)
    far_slow = partner_2(chosen_slow, "rep", 1)

    def last_work():
        _, saved = forward_rows(arrived, gate_w, up_w, down_w)
        term, back = backward_rows(own_data, arrived, saved, gate_w, up_w, down_w)
        return term, back

    def last_idle():
        return jnp.zeros((hidden_units, model_width), jnp.float32), own_data

    last_term, back = lax.cond(on_first, last_idle, last_work)
    back = cut(back)
    returned = [send_rows(back[b], flip_keys[b], 1) for b in range(micro_count)]
    far_slow, *returned = lax.optimization_barrier((far_slow, *returned))
    returned = jnp.concatenate(returned)
    partner_slow = jnp.where(flip_bits >> 1 & 1 == 1, far_slow, chosen_slow)
    grad_sum = lax.cond(
        on_first, lambda: grad_rows(returned, hidden, hidden_units), lambda: last_term
    )
    masks = jnp.zeros((8, model_width), jnp.int32)
    masks = masks.at[0].set(flip_bits & 1).at[1].set(flip_bits >> 1 & 1)
    new_slow, new_momentum = outer_update(
        masks, grad_sum, adam_m[0, 0], adam_v[0, 0], down_w, partner_slow, momentum[0, 0]
    )
    return new_slow[None, None], new_momentum[None, None]


def solution(mesh):
    placed = (
        P("section", "rep", None, None, None),
        P("section", "rep", None, None),
        P("section", "rep", None, None),
        P("section", "rep", None, None),
        P("section", "rep", None, None),
        P("section", "rep", None, None),
        P("section", "rep", None, None),
        P(),
        P(),
    )

    return jax.shard_map(
        on_device,
        mesh=mesh,
        in_specs=placed,
        out_specs=(P("section", "rep", None, None), P("section", "rep", None, None)),
        check_vma=False,
    )
```

profile of v0, /device:TPU:0, one launch (start us, length us, event | category | flops | bytes accessed | tf_op | source)
XLA Modules:
  0.0 82.7 jit_solution(12997822913556358915)
XLA Ops:
  0.6 1.1 %copy.89 = bf16[1,1,2,128,1024]{4,3,2,1,0:T(8,128)(2,1)S(1)} copy(bf16[1,1,2,128,1024]{4,3,2,1,0:T(8,128)(2,1)} %param.83) | data formatting | bytes 1048576
  1.8 0.1 copy-done.3
  1.9 3.0 %collective-permute-start.64 = (bf16[256,1024]{1,0:T(8,128)(2,1)S(1)}, bf16[256,1024]{1,0:T(8,128)(2,1)S(1)}, u32[]{:S(2)}, u32[]{:S(2)}) collective-permute-start(bf16[256,1024]{1,0:T(8,128)(2,1)S(1)} %bitcast.36), channel_id=1, source_target_pairs={{0,2},{2,0},{4,6},{6,4},{8,10},{10,8},{12,14},{14,12},{16,18},{18,... | collective-permute-start | bytes 1572872 | tf_op jit(solution)/shard_map/ppermute | solution.py:12
  4.9 0.7 copy-done.8
  5.5 0.5 fusion.24
  7.4 0.0 copy-start.9
  7.4 0.6 copy-done.9
  8.0 0.6 dynamic_slice.3
  9.3 3.5 %conditional.7 = (bf16[256,1024]{1,0:T(8,128)(2,1)S(1)}, bf16[256,256]{1,0:T(8,128)(2,1)}) conditional(s32[]{:T(128)} %convert_element_type.39, bf16[256,1024]{1,0:T(8,128)(2,1)S(1)} %bitcast.32, (bf16[256,1024]{1,0:T(8,128)(2,1)S(1)}, bf16[1024,256]{1,0:T(8,128)(2,1)S(1)}, bf16[1024,256]{1,0:T(8,128)(2,1)}, bf16[256,1024]{1,0:T(8,128)(2,1)S(1)}) %tuple.327), branch_computations={%region_0.0_spmd, %region_1.3_spmd} | conditional | flops 406585600 | bytes 7083052 | solution.py:227
  9.3 0.2 fusion.3
  9.5 0.0 copy-start.7
  9.5 0.3 convolution_multiply_fusion.2
  9.9 0.7 copy-done.7
  10.5 1.0 %fusion.2 = bf16[256,256]{1,0:T(8,128)(2,1)} fusion(bf16[1024,256]{1,0:T(8,128)(2,1)S(1)} %copy-done.7, f32[256,256]{1,0:T(8,128)S(1)} %convolution_multiply_fusion.2, bf16[256,1024]{1,0:T(8,128)(2,1)S(1)} %get-tuple-element.185, f32[256]{0:T(256)S(1)} %add_rsqrt_fusion), kind=kOutput, calls=%fused_computation.8 | convolution fusion | flops 135462912 | bytes 1442816 | tf_op jit(solution)/shard_map/cond/branch_1_fun/dot_general | solution.py:22
  11.5 1.2 %fusion = bf16[256,1024]{1,0:T(8,128)(2,1)S(1)} fusion(bf16[256,256]{1,0:T(8,128)(2,1)} %fusion.2, bf16[256,1024]{1,0:T(8,128)(2,1)S(1)} %get-tuple-element.188, bf16[256,1024]{1,0:T(8,128)(2,1)S(1)} %get-tuple-element.185), kind=kOutput, calls=%fused_computation.4 | convolution fusion | flops 135266304 | bytes 1703936 | tf_op jit(solution)/shard_map/cond/branch_1_fun/dot_general | solution.py:24
  12.8 6.8 %conditional.8 = (bf16[128,1024]{1,0:T(8,128)(2,1)}) conditional(s32[]{:T(128)} %bitcast.4, bf16[128,1024]{1,0:T(8,128)(2,1)S(1)} %get-tuple-element.230, bf16[128,1024]{1,0:T(8,128)(2,1)S(1)} %get-tuple-element.230, bf16[128,1024]{1,0:T(8,128)(2,1)S(1)} %get-tuple-element.230, ...), branch_computations={%region_3.4_spmd, %region_4.5_spmd, %region_5.6_spmd, %region_6.7_... | conditional | bytes 1048624 | solution.py:82
  12.8 3.5 %collective-permute-start.15 = (bf16[128,1024]{1,0:T(8,128)(2,1)S(1)}, bf16[128,1024]{1,0:T(8,128)(2,1)}, u32[]{:S(2)}, u32[]{:S(2)}) collective-permute-start(bf16[128,1024]{1,0:T(8,128)(2,1)S(1)} %param.21), channel_id=1, source_target_pairs={{0,31},{2,29},{4,27},{6,25},{8,23},{10,21},{12,19},{14,17},{16,15}... | collective-permute-start | bytes 786440 | tf_op jit(solution)/shard_map/cond/branch_15_fun/ppermute | solution.py:78
  16.4 3.2 %collective-permute-done.15 = bf16[128,1024]{1,0:T(8,128)(2,1)} collective-permute-done((bf16[128,1024]{1,0:T(8,128)(2,1)S(1)}, bf16[128,1024]{1,0:T(8,128)(2,1)}, u32[]{:S(2)}, u32[]{:S(2)}) %collective-permute-start.15) | collective-permute-done | bytes 262176 | tf_op jit(solution)/shard_map/cond/branch_15_fun/ppermute | solution.py:78
  19.6 10.3 %conditional.9 = (bf16[128,1024]{1,0:T(8,128)(2,1)}) conditional(s32[]{:T(128)} %bitcast.7, bf16[128,1024]{1,0:T(8,128)(2,1)S(1)} %get-tuple-element.229, bf16[128,1024]{1,0:T(8,128)(2,1)S(1)} %get-tuple-element.229, bf16[128,1024]{1,0:T(8,128)(2,1)S(1)} %get-tuple-element.229, ...), branch_computations={%region_19.20_spmd, %region_20.21_spmd, %region_21.22_spmd, %regio... | conditional | bytes 1048624 | solution.py:82
  19.6 7.1 %collective-permute-start.17 = (bf16[128,1024]{1,0:T(8,128)(2,1)S(1)}, bf16[128,1024]{1,0:T(8,128)(2,1)}, u32[]{:S(2)}, u32[]{:S(2)}) collective-permute-start(bf16[128,1024]{1,0:T(8,128)(2,1)S(1)} %param.23), channel_id=1, source_target_pairs={{0,3},{2,1},{4,7},{6,5},{8,11},{10,9},{12,15},{14,13},{16,19},{18,... | collective-permute-start | bytes 786440 | tf_op jit(solution)/shard_map/cond/branch_1_fun/ppermute | solution.py:78
  26.7 3.2 %collective-permute-done.17 = bf16[128,1024]{1,0:T(8,128)(2,1)} collective-permute-done((bf16[128,1024]{1,0:T(8,128)(2,1)S(1)}, bf16[128,1024]{1,0:T(8,128)(2,1)}, u32[]{:S(2)}, u32[]{:S(2)}) %collective-permute-start.17) | collective-permute-done | bytes 262176 | tf_op jit(solution)/shard_map/cond/branch_1_fun/ppermute | solution.py:78
  29.9 0.0 collective-permute-done.64
  29.9 0.1 broadcast_select_fusion.1
  30.0 0.6 collective-permute-start.65
  30.5 0.1 scatter.13
  30.6 0.1 scatter.14.masks
  30.7 0.0 copy-start.6
  30.7 1.1 %pad_maximum_fusion = bf16[256,1024]{1,0:T(8,128)(2,1)S(1)} fusion(bf16[128,1024]{1,0:T(8,128)(2,1)} %get-tuple-element.248, bf16[128,1024]{1,0:T(8,128)(2,1)} %get-tuple-element.247), kind=kLoop, calls=%fused_computation.43 | loop fusion | flops 1048576 | bytes 1048576 | tf_op jit(solution)/shard_map/concatenate | solution.py:231
  31.9 0.1 copy-done.6
  31.9 0.1 conditional.10
  31.9 0.1 broadcast.117
  32.1 0.9 %copy-done.4 = f32[256,1024]{1,0:T(8,128)} copy-done((f32[256,1024]{1,0:T(8,128)}, f32[256,1024]{1,0:T(8,128)S(1)}, u32[]{:S(2)}) %copy-start.4) | copy-done | bytes 1048600
  33.0 11.5 %conditional.11 = (bf16[128,1024]{1,0:T(8,128)(2,1)}) conditional(s32[]{:T(128)} %bitcast.4, bf16[128,1024]{1,0:T(8,128)(2,1)S(1)} %get-tuple-element.228, bf16[128,1024]{1,0:T(8,128)(2,1)S(1)} %get-tuple-element.228, bf16[128,1024]{1,0:T(8,128)(2,1)S(1)} %get-tuple-element.228, ...), branch_computations={%region_39.40_spmd, %region_40.41_spmd, %region_41.42_spmd, %regio... | conditional | bytes 1048624 | solution.py:82
  33.0 1.3 %collective-permute-start.47 = (bf16[128,1024]{1,0:T(8,128)(2,1)S(1)}, bf16[128,1024]{1,0:T(8,128)(2,1)}, u32[]{:S(2)}, u32[]{:S(2)}) collective-permute-start(bf16[128,1024]{1,0:T(8,128)(2,1)S(1)} %param.55), channel_id=1, source_target_pairs={{1,30},{3,28},{5,26},{7,24},{9,22},{11,20},{13,18},{15,16},{17,14}... | collective-permute-start | bytes 786440 | tf_op jit(solution)/shard_map/cond/branch_15_fun/ppermute | solution.py:78
  34.3 10.2 %collective-permute-done.47 = bf16[128,1024]{1,0:T(8,128)(2,1)} collective-permute-done((bf16[128,1024]{1,0:T(8,128)(2,1)S(1)}, bf16[128,1024]{1,0:T(8,128)(2,1)}, u32[]{:S(2)}, u32[]{:S(2)}) %collective-permute-start.47) | collective-permute-done | bytes 262176 | tf_op jit(solution)/shard_map/cond/branch_15_fun/ppermute | solution.py:78
  44.5 7.8 %conditional.12 = (bf16[128,1024]{1,0:T(8,128)(2,1)}) conditional(s32[]{:T(128)} %bitcast.7, bf16[128,1024]{1,0:T(8,128)(2,1)S(1)} %get-tuple-element.227, bf16[128,1024]{1,0:T(8,128)(2,1)S(1)} %get-tuple-element.227, bf16[128,1024]{1,0:T(8,128)(2,1)S(1)} %get-tuple-element.227, ...), branch_computations={%region_55.56_spmd, %region_56.57_spmd, %region_57.58_spmd, %regio... | conditional | bytes 1048624 | solution.py:82
  44.5 1.3 %collective-permute-start.49 = (bf16[128,1024]{1,0:T(8,128)(2,1)S(1)}, bf16[128,1024]{1,0:T(8,128)(2,1)}, u32[]{:S(2)}, u32[]{:S(2)}) collective-permute-start(bf16[128,1024]{1,0:T(8,128)(2,1)S(1)} %param.57), channel_id=1, source_target_pairs={{1,2},{3,0},{5,6},{7,4},{9,10},{11,8},{13,14},{15,12},{17,18},{19,... | collective-permute-start | bytes 786440 | tf_op jit(solution)/shard_map/cond/branch_1_fun/ppermute | solution.py:78
  45.8 6.5 %collective-permute-done.49 = bf16[128,1024]{1,0:T(8,128)(2,1)} collective-permute-done((bf16[128,1024]{1,0:T(8,128)(2,1)S(1)}, bf16[128,1024]{1,0:T(8,128)(2,1)}, u32[]{:S(2)}, u32[]{:S(2)}) %collective-permute-start.49) | collective-permute-done | bytes 262176 | tf_op jit(solution)/shard_map/cond/branch_1_fun/ppermute | solution.py:78
  52.3 0.0 collective-permute-done.65
  52.3 1.4 %pad_maximum_fusion.1 = (bf16[256,1024]{1,0:T(8,128)(2,1)S(1)}, bf16[256,1024]{1,0:T(8,128)(2,1)S(1)}) fusion(bf16[128,1024]{1,0:T(8,128)(2,1)} %get-tuple-element.250, bf16[128,1024]{1,0:T(8,128)(2,1)} %get-tuple-element.249, bf16[256,1024]{1,0:T(8,128)(2,1)} %collective-permute-done.65, bf16[256,1024]{1,0:T(8,128)(2,1)S(1)} %broadcast_select_fusion.1, ...), kind=kLoop, calls=%fused_computation.44 | loop fusion | flops 1310720 | bytes 2621441 | tf_op jit(solution)/shard_map/concatenate | solution.py:247
  53.7 0.0 copy-start
  53.7 0.0 copy-start.1
  53.8 0.0 copy-start.2
  53.8 2.3 %conditional.13 = (f32[256,1024]{1,0:T(8,128)}) conditional(s32[]{:T(128)} %convert_element_type.39, f32[256,1024]{1,0:T(8,128)} %copy-done.4, (bf16[256,256]{1,0:T(8,128)(2,1)}, bf16[256,1024]{1,0:T(8,128)(2,1)S(1)}) %tuple.240), branch_computations={%region_71.72_spmd, %region_72.73_spmd} | conditional | flops 134479872 | bytes 1703944 | solution.py:249
  53.8 2.3 %convolution_multiply_fusion.7 = f32[256,1024]{1,0:T(8,128)} fusion(bf16[256,256]{1,0:T(8,128)(2,1)} %get-tuple-element.194, bf16[256,1024]{1,0:T(8,128)(2,1)S(1)} %get-tuple-element.195), kind=kOutput, calls=%fused_computation.42 | convolution fusion | flops 134479872 | bytes 1703936 | tf_op jit(solution)/shard_map/cond/branch_1_fun/dot_general | solution.py:36
  56.1 25.0 %outer.1 = (bf16[256,1024]{1,0:T(8,128)(2,1)S(1)}, bf16[256,1024]{1,0:T(8,128)(2,1)S(1)}) custom-call(s32[8,1024]{1,0:T(8,128)S(1)} %scatter.14.masks, f32[256,1024]{1,0:T(8,128)} %get-tuple-element.251.grad, bf16[256,1024]{1,0:T(8,128)(2,1)S(1)} %bitcast.27, bf16[256,1024]{1,0:T(8,128)(2,1)S(1)} %bitcast.28, bf16[256,1024]{1,0:T(8,128)(2,1)S(1)} %bitcast.39, ...), custom_call_target="tpu_custom_call" | custom-call | tf_op jit(solution)/shard_map/outer/pallas_call | solution.py:191
  81.2 0.8 copy.90
  82.0 0.8 copy.91
  (13 shorter events, 0.1 us)
Async XLA Ops:
  0.6 8.6 %copy-start.5 = (bf16[1,1,1024,256]{3,2,1,0:T(8,128)(2,1)S(1)}, bf16[1,1,1024,256]{3,2,1,0:T(8,128)(2,1)}, u32[]{:S(2)}) copy-start(bf16[1,1,1024,256]{3,2,1,0:T(8,128)(2,1)} %param.84) | copy-start | bytes 1572868
  0.6 1.3 %copy-start.3 = (bf16[1,1,256,1024]{3,2,1,0:T(8,128)(2,1)S(1)}, bf16[1,1,256,1024]{3,2,1,0:T(8,128)(2,1)}, u32[]{:S(2)}) copy-start(bf16[1,1,256,1024]{3,2,1,0:T(8,128)(2,1)} %param.86) | copy-start | bytes 1572868
  1.9 28.0 %collective-permute-start.64 = (bf16[256,1024]{1,0:T(8,128)(2,1)S(1)}, bf16[256,1024]{1,0:T(8,128)(2,1)S(1)}, u32[]{:S(2)}, u32[]{:S(2)}) collective-permute-start(bf16[256,1024]{1,0:T(8,128)(2,1)S(1)} %bitcast.36), channel_id=1, source_target_pairs={{0,2},{2,0},{4,6},{6,4},{8,10},{10,8},{12,14},{14,12},{16,18},{18,... | collective-permute-start | bytes 1572872 | tf_op jit(solution)/shard_map/ppermute | solution.py:12
  4.9 0.7 copy-start.8
  7.4 0.7 copy-start.9
  9.5 1.0 %copy-start.7 = (bf16[1024,256]{1,0:T(8,128)(2,1)S(1)}, bf16[1024,256]{1,0:T(8,128)(2,1)}, u32[]{:S(2)}) copy-start(bf16[1024,256]{1,0:T(8,128)(2,1)} %get-tuple-element.187) | copy-start | bytes 1572868 | tf_op jit(solution)/shard_map/cond
  12.8 6.7 %collective-permute-start.15 = (bf16[128,1024]{1,0:T(8,128)(2,1)S(1)}, bf16[128,1024]{1,0:T(8,128)(2,1)}, u32[]{:S(2)}, u32[]{:S(2)}) collective-permute-start(bf16[128,1024]{1,0:T(8,128)(2,1)S(1)} %param.21), channel_id=1, source_target_pairs={{0,31},{2,29},{4,27},{6,25},{8,23},{10,21},{12,19},{14,17},{16,15}... | collective-permute-start | bytes 786440 | tf_op jit(solution)/shard_map/cond/branch_15_fun/ppermute | solution.py:78
  19.6 10.3 %collective-permute-start.17 = (bf16[128,1024]{1,0:T(8,128)(2,1)S(1)}, bf16[128,1024]{1,0:T(8,128)(2,1)}, u32[]{:S(2)}, u32[]{:S(2)}) collective-permute-start(bf16[128,1024]{1,0:T(8,128)(2,1)S(1)} %param.23), channel_id=1, source_target_pairs={{0,3},{2,1},{4,7},{6,5},{8,11},{10,9},{12,15},{14,13},{16,19},{18,... | collective-permute-start | bytes 786440 | tf_op jit(solution)/shard_map/cond/branch_1_fun/ppermute | solution.py:78
  30.0 22.3 %collective-permute-start.65 = (bf16[256,1024]{1,0:T(8,128)(2,1)S(1)}, bf16[256,1024]{1,0:T(8,128)(2,1)}, u32[]{:S(2)}, u32[]{:S(2)}) collective-permute-start(bf16[256,1024]{1,0:T(8,128)(2,1)S(1)} %broadcast_select_fusion.1), channel_id=1, source_target_pairs={{0,4},{2,6},{4,0},{6,2},{8,12},{10,14},{12,8},{14,10},{16,20},{18,... | collective-permute-start | bytes 1572872 | tf_op jit(solution)/shard_map/ppermute | solution.py:12
  30.7 1.2 %copy-start.6 = (bf16[1,1,1024,256]{3,2,1,0:T(8,128)(2,1)S(1)}, bf16[1,1,1024,256]{3,2,1,0:T(8,128)(2,1)}, u32[]{:S(2)}) copy-start(bf16[1,1,1024,256]{3,2,1,0:T(8,128)(2,1)} %param.85) | copy-start | bytes 1572868
  32.0 1.0 %copy-start.4 = (f32[256,1024]{1,0:T(8,128)}, f32[256,1024]{1,0:T(8,128)S(1)}, u32[]{:S(2)}) copy-start(f32[256,1024]{1,0:T(8,128)S(1)} %get-tuple-element.213) | copy-start | bytes 3145732
  33.0 11.5 %collective-permute-start.47 = (bf16[128,1024]{1,0:T(8,128)(2,1)S(1)}, bf16[128,1024]{1,0:T(8,128)(2,1)}, u32[]{:S(2)}, u32[]{:S(2)}) collective-permute-start(bf16[128,1024]{1,0:T(8,128)(2,1)S(1)} %param.55), channel_id=1, source_target_pairs={{1,30},{3,28},{5,26},{7,24},{9,22},{11,20},{13,18},{15,16},{17,14}... | collective-permute-start | bytes 786440 | tf_op jit(solution)/shard_map/cond/branch_15_fun/ppermute | solution.py:78
  44.5 7.8 %collective-permute-start.49 = (bf16[128,1024]{1,0:T(8,128)(2,1)S(1)}, bf16[128,1024]{1,0:T(8,128)(2,1)}, u32[]{:S(2)}, u32[]{:S(2)}) collective-permute-start(bf16[128,1024]{1,0:T(8,128)(2,1)S(1)} %param.57), channel_id=1, source_target_pairs={{1,2},{3,0},{5,6},{7,4},{9,10},{11,8},{13,14},{15,12},{17,18},{19,... | collective-permute-start | bytes 786440 | tf_op jit(solution)/shard_map/cond/branch_1_fun/ppermute | solution.py:78
  53.7 2.4 %copy-start = (bf16[1,1,256,1024]{3,2,1,0:T(8,128)(2,1)S(1)}, bf16[1,1,256,1024]{3,2,1,0:T(8,128)(2,1)}, u32[]{:S(2)}) copy-start(bf16[1,1,256,1024]{3,2,1,0:T(8,128)(2,1)} %param.87) | copy-start | bytes 1572868
  53.7 2.4 %copy-start.1 = (bf16[1,1,256,1024]{3,2,1,0:T(8,128)(2,1)S(1)}, bf16[1,1,256,1024]{3,2,1,0:T(8,128)(2,1)}, u32[]{:S(2)}) copy-start(bf16[1,1,256,1024]{3,2,1,0:T(8,128)(2,1)} %param.88) | copy-start | bytes 1572868
  53.8 2.4 %copy-start.2 = (bf16[1,1,256,1024]{3,2,1,0:T(8,128)(2,1)S(1)}, bf16[1,1,256,1024]{3,2,1,0:T(8,128)(2,1)}, u32[]{:S(2)}) copy-start(bf16[1,1,256,1024]{3,2,1,0:T(8,128)(2,1)} %param.89) | copy-start | bytes 1572868
where the time goes:
time: 83.5 us; the launch traced here: 82.7 us
  Pallas kernels  25 us (30%)
  waiting for transfers between devices  23.1 us (28%)
  starting transfers between devices  16.8 us (20%)
  local copies, waits for them, and re-layouts  7.32 us (9%)
  matrix products  4.89 us (6%)
  other arithmetic  2.81 us (3%)
  between operations  2.74 us (3%)
    pallas_call x1, Pallas kernels, outer_update(): pl.pallas_call(functools.partial(outer_kernel, chunks), out_shape=(out, o...  25 us
    ppermute x4, waiting for transfers between devices, run(): return lax.ppermute(rows, ('rep', 'section'), pairs)  23.1 us
    ppermute x4, starting transfers between devices, run(): return lax.ppermute(rows, ('rep', 'section'), pairs)  13.2 us
    unnamed x21, local copies, waits for them, and re-layouts  5.19 us
    ppermute x2, starting transfers between devices, partner_2(): lax.ppermute(x, axis, [(i, i ^ 1 << bit) for i in range(lax.axis_size(axi...  3.54 us
    dot_general x1, matrix products, grad_rows(): lax.dot_general(hidden, cotangent, (((0,), (0,)), ((), ())), preferred_el...  2.32 us
  transfers between devices with their start and end apart: 6, of which 4 were waited for; matrix products, arithmetic and copies ran while one was open for 6% of the time, Pallas kernels for 0%

commit v1 on v0

--- a/solution.py
+++ b/solution.py
@@ -103,18 +103,18 @@
     def part(c):
         return pl.ds(pl.multiple_of(c * rows, rows), rows)
 
-    def near_copy(c):
+    def near_copy(c, order):
         return pltpu.make_async_remote_copy(
             src_ref=own.at[part(c)], dst_ref=near.at[part(c)],
             send_sem=send_near.at[c], recv_sem=recv_near.at[c],
-            device_id={"rep": peers[0]}, device_id_type=pl.DeviceIdType.MESH,
-        )
-
-    def far_copy(c):
+            device_id={"rep": peers[order]}, device_id_type=pl.DeviceIdType.MESH,
+        )
+
+    def far_copy(c, order):
         return pltpu.make_async_remote_copy(
             src_ref=chosen.at[part(c)], dst_ref=far.at[part(c)],
             send_sem=send_far.at[c], recv_sem=recv_far.at[c],
-            device_id={"rep": peers[1]}, device_id_type=pl.DeviceIdType.MESH,
+            device_id={"rep": peers[1 - order]}, device_id_type=pl.DeviceIdType.MESH,
         )
 
     def adam(c):
@@ -125,65 +125,60 @@
         step = first / (jnp.sqrt(second) + 1e-08)
         own[p, :] = (step + 0.1 * slow[p, :].astype(f32)).astype(bf16)
 
-    adam(0)
-    pl.semaphore_wait(barrier, 2)
-    near_copy(0).start()
-
-    def begin(c, carry):
+    def send(c, order):
+        near_copy(c, order).start()
+
+    def begin(c, order):
         adam(c)
-        near_copy(c).start()
-        return carry
-
-    lax.fori_loop(1, chunks, begin, 0)
-
-    def pass_on(c):
+        send(c, order)
+
+    def pass_on(c, order):
         p = part(c)
-        near_copy(c).wait_recv()
+        near_copy(c, order).wait_recv()
         chosen[p, :] = jnp.where(
-            masks[0:1, :] == 1, near[p, :].astype(f32), own[p, :].astype(f32)
+            masks[order : order + 1, :] == 1, near[p, :].astype(f32), own[p, :].astype(f32)
         ).astype(bf16)
-        far_copy(c).start()
-
-    def finish(c):
+        far_copy(c, order).start()
+
+    def finish(c, order):
         p = part(c)
-        far_copy(c).wait_recv()
-        mate = jnp.where(masks[1:2, :] == 1, far[p, :].astype(f32), chosen[p, :].astype(f32))
+        far_copy(c, order).wait_recv()
+        mate = jnp.where(
+            masks[1 - order : 2 - order, :] == 1, far[p, :].astype(f32), chosen[p, :].astype(f32)
+        )
         mean = 0.5 * (own[p, :].astype(f32) + mate)
         moment = 0.9 * momentum[p, :].astype(f32) + mean
         averaged = 0.5 * (slow[p, :].astype(f32) + mate_slow[p, :].astype(f32))
         new_slow[p, :] = (averaged - 0.014 * (0.9 * moment + mean)).astype(bf16)
         new_momentum[p, :] = moment.astype(bf16)
 
-    lag = 2
-
-    def steady(c, carry):
-        pass_on(c)
-
-        @pl.when(c >= lag)
-        def _():
-            finish(c - lag)
-
-        return carry
-
-    lax.fori_loop(0, chunks, steady, 0)
-
-    def drain(c, carry):
-        finish(c)
-        return carry
-
-    lax.fori_loop(chunks - lag, chunks, drain, 0)
-
-    def settle(c, carry):
-        near_copy(c).wait_send()
-        far_copy(c).wait_send()
-        return carry
-
-    lax.fori_loop(0, chunks, settle, 0)
+    def settle(c, order):
+        near_copy(c, order).wait_send()
+        far_copy(c, order).wait_send()
+
+    def both(start, stop, *stages):
+        def run(pair, carry):
+            for stage in stages:
+                for order in range(2):
+                    stage(2 * pair + order, order)
+            return carry
+
+        lax.fori_loop(start, stop, run, 0)
+
+    pairs = chunks // 2
+    both(0, 1, lambda c, order: adam(c))
+    pl.semaphore_wait(barrier, 2)
+    both(0, 1, send)
+    both(1, pairs, begin)
+    both(0, 1, pass_on)
+    both(1, pairs, pass_on, lambda c, order: finish(c - 2, order))
+    both(pairs - 1, pairs, finish)
+    both(0, pairs, settle)
 
 
 def outer_update(masks, grad, first_in, second_in, slow, mate_slow, momentum):
     hidden_units, model_width = grad.shape
-    chunks = hidden_units // 16
+    chunks = hidden_units // 32
     block = pltpu.VMEM((hidden_units, model_width), jnp.bfloat16)
     sems = pltpu.SemaphoreType.DMA((chunks,))
     out = jax.ShapeDtypeStruct((hidden_units, model_width), jnp.bfloat16)

time: 83.5 us -> 74.1 us (0.89)
  Pallas kernels: 25 us -> 15.7 us
    pallas_call x1, Pallas kernels: 25 us -> 15.7 us  [outer_update(): pl.pallas_call(functools.partial(outer_kernel, chunks), out_shape=(out, o...]
  transfers between devices with their start and end apart: 6 -> 6, of which waited for: 4 -> 4; matrix products, arithmetic and copies ran while one was open for 6% -> 7% of each run, Pallas kernels for 0% -> 0%
where the time goes in v1:
time: 74.1 us; the launch traced here: 73.4 us
  waiting for transfers between devices  23.1 us (31%)
  starting transfers between devices  16.8 us (23%)
  Pallas kernels  15.7 us (21%)
  local copies, waits for them, and re-layouts  7.32 us (10%)
  matrix products  4.89 us (7%)
  other arithmetic  2.81 us (4%)
  between operations  2.74 us (4%)
    ppermute x4, waiting for transfers between devices, run(): return lax.ppermute(rows, ('rep', 'section'), pairs)  23.1 us
    pallas_call x1, Pallas kernels, outer_update(): pl.pallas_call(functools.partial(outer_kernel, chunks), out_shape=(out, o...  15.7 us
    ppermute x4, starting transfers between devices, run(): return lax.ppermute(rows, ('rep', 'section'), pairs)  13.2 us
    unnamed x21, local copies, waits for them, and re-layouts  5.19 us
    ppermute x2, starting transfers between devices, partner_2(): lax.ppermute(x, axis, [(i, i ^ 1 << bit) for i in range(lax.axis_size(axi...  3.54 us
    dot_general x1, matrix products, grad_rows(): lax.dot_general(hidden, cotangent, (((0,), (0,)), ((), ())), preferred_el...  2.32 us
  transfers between devices with their start and end apart: 6, of which 4 were waited for; matrix products, arithmetic and copies ran while one was open for 7% of the time, Pallas kernels for 0%

profile of v1, /device:TPU:0, one launch (start us, length us, event | category | flops | bytes accessed | tf_op | source)
XLA Modules:
  0.0 73.4 jit_solution(8214899845138367148)
XLA Ops:
  0.6 1.1 %copy.89 = bf16[1,1,2,128,1024]{4,3,2,1,0:T(8,128)(2,1)S(1)} copy(bf16[1,1,2,128,1024]{4,3,2,1,0:T(8,128)(2,1)} %param.83) | data formatting | bytes 1048576
  1.8 0.1 copy-done.3
  1.9 3.0 %collective-permute-start.64 = (bf16[256,1024]{1,0:T(8,128)(2,1)S(1)}, bf16[256,1024]{1,0:T(8,128)(2,1)S(1)}, u32[]{:S(2)}, u32[]{:S(2)}) collective-permute-start(bf16[256,1024]{1,0:T(8,128)(2,1)S(1)} %bitcast.36), channel_id=1, source_target_pairs={{0,2},{2,0},{4,6},{6,4},{8,10},{10,8},{12,14},{14,12},{16,18},{18,... | collective-permute-start | bytes 1572872 | tf_op jit(solution)/shard_map/ppermute | solution.py:12
  4.9 0.7 copy-done.8
  5.5 0.5 fusion.24
  7.4 0.0 copy-start.9
  7.4 0.6 copy-done.9
  8.0 0.6 dynamic_slice.3
  9.3 3.5 %conditional.7 = (bf16[256,1024]{1,0:T(8,128)(2,1)S(1)}, bf16[256,256]{1,0:T(8,128)(2,1)}) conditional(s32[]{:T(128)} %convert_element_type.39, bf16[256,1024]{1,0:T(8,128)(2,1)S(1)} %bitcast.32, (bf16[256,1024]{1,0:T(8,128)(2,1)S(1)}, bf16[1024,256]{1,0:T(8,128)(2,1)S(1)}, bf16[1024,256]{1,0:T(8,128)(2,1)}, bf16[256,1024]{1,0:T(8,128)(2,1)S(1)}) %tuple.327), branch_computations={%region_0.0_spmd, %region_1.3_spmd} | conditional | flops 406585600 | bytes 7083052 | solution.py:222
  9.3 0.2 fusion.3
  9.5 0.0 copy-start.7
  9.5 0.3 convolution_multiply_fusion.2
  9.9 0.7 copy-done.7
  10.5 1.0 %fusion.2 = bf16[256,256]{1,0:T(8,128)(2,1)} fusion(bf16[1024,256]{1,0:T(8,128)(2,1)S(1)} %copy-done.7, f32[256,256]{1,0:T(8,128)S(1)} %convolution_multiply_fusion.2, bf16[256,1024]{1,0:T(8,128)(2,1)S(1)} %get-tuple-element.185, f32[256]{0:T(256)S(1)} %add_rsqrt_fusion), kind=kOutput, calls=%fused_computation.8 | convolution fusion | flops 135462912 | bytes 1442816 | tf_op jit(solution)/shard_map/cond/branch_1_fun/dot_general | solution.py:22
  11.5 1.2 %fusion = bf16[256,1024]{1,0:T(8,128)(2,1)S(1)} fusion(bf16[256,256]{1,0:T(8,128)(2,1)} %fusion.2, bf16[256,1024]{1,0:T(8,128)(2,1)S(1)} %get-tuple-element.188, bf16[256,1024]{1,0:T(8,128)(2,1)S(1)} %get-tuple-element.185), kind=kOutput, calls=%fused_computation.4 | convolution fusion | flops 135266304 | bytes 1703936 | tf_op jit(solution)/shard_map/cond/branch_1_fun/dot_general | solution.py:24
  12.8 6.8 %conditional.8 = (bf16[128,1024]{1,0:T(8,128)(2,1)}) conditional(s32[]{:T(128)} %bitcast.4, bf16[128,1024]{1,0:T(8,128)(2,1)S(1)} %get-tuple-element.230, bf16[128,1024]{1,0:T(8,128)(2,1)S(1)} %get-tuple-element.230, bf16[128,1024]{1,0:T(8,128)(2,1)S(1)} %get-tuple-element.230, ...), branch_computations={%region_3.4_spmd, %region_4.5_spmd, %region_5.6_spmd, %region_6.7_... | conditional | bytes 1048624 | solution.py:82
  12.8 3.5 %collective-permute-start.15 = (bf16[128,1024]{1,0:T(8,128)(2,1)S(1)}, bf16[128,1024]{1,0:T(8,128)(2,1)}, u32[]{:S(2)}, u32[]{:S(2)}) collective-permute-start(bf16[128,1024]{1,0:T(8,128)(2,1)S(1)} %param.21), channel_id=1, source_target_pairs={{0,31},{2,29},{4,27},{6,25},{8,23},{10,21},{12,19},{14,17},{16,15}... | collective-permute-start | bytes 786440 | tf_op jit(solution)/shard_map/cond/branch_15_fun/ppermute | solution.py:78
  16.4 3.2 %collective-permute-done.15 = bf16[128,1024]{1,0:T(8,128)(2,1)} collective-permute-done((bf16[128,1024]{1,0:T(8,128)(2,1)S(1)}, bf16[128,1024]{1,0:T(8,128)(2,1)}, u32[]{:S(2)}, u32[]{:S(2)}) %collective-permute-start.15) | collective-permute-done | bytes 262176 | tf_op jit(solution)/shard_map/cond/branch_15_fun/ppermute | solution.py:78
  19.6 10.3 %conditional.9 = (bf16[128,1024]{1,0:T(8,128)(2,1)}) conditional(s32[]{:T(128)} %bitcast.7, bf16[128,1024]{1,0:T(8,128)(2,1)S(1)} %get-tuple-element.229, bf16[128,1024]{1,0:T(8,128)(2,1)S(1)} %get-tuple-element.229, bf16[128,1024]{1,0:T(8,128)(2,1)S(1)} %get-tuple-element.229, ...), branch_computations={%region_19.20_spmd, %region_20.21_spmd, %region_21.22_spmd, %regio... | conditional | bytes 1048624 | solution.py:82
  19.6 7.1 %collective-permute-start.17 = (bf16[128,1024]{1,0:T(8,128)(2,1)S(1)}, bf16[128,1024]{1,0:T(8,128)(2,1)}, u32[]{:S(2)}, u32[]{:S(2)}) collective-permute-start(bf16[128,1024]{1,0:T(8,128)(2,1)S(1)} %param.23), channel_id=1, source_target_pairs={{0,3},{2,1},{4,7},{6,5},{8,11},{10,9},{12,15},{14,13},{16,19},{18,... | collective-permute-start | bytes 786440 | tf_op jit(solution)/shard_map/cond/branch_1_fun/ppermute | solution.py:78
  26.7 3.2 %collective-permute-done.17 = bf16[128,1024]{1,0:T(8,128)(2,1)} collective-permute-done((bf16[128,1024]{1,0:T(8,128)(2,1)S(1)}, bf16[128,1024]{1,0:T(8,128)(2,1)}, u32[]{:S(2)}, u32[]{:S(2)}) %collective-permute-start.17) | collective-permute-done | bytes 262176 | tf_op jit(solution)/shard_map/cond/branch_1_fun/ppermute | solution.py:78
  29.9 0.0 collective-permute-done.64
  29.9 0.1 broadcast_select_fusion.1
  30.0 0.6 collective-permute-start.65
  30.5 0.1 scatter.13
  30.6 0.1 scatter.14.masks
  30.7 0.0 copy-start.6
  30.7 1.1 %pad_maximum_fusion = bf16[256,1024]{1,0:T(8,128)(2,1)S(1)} fusion(bf16[128,1024]{1,0:T(8,128)(2,1)} %get-tuple-element.248, bf16[128,1024]{1,0:T(8,128)(2,1)} %get-tuple-element.247), kind=kLoop, calls=%fused_computation.43 | loop fusion | flops 1048576 | bytes 1048576 | tf_op jit(solution)/shard_map/concatenate | solution.py:226
  31.9 0.1 copy-done.6
  31.9 0.1 conditional.10
  31.9 0.1 broadcast.117
  32.1 0.9 %copy-done.4 = f32[256,1024]{1,0:T(8,128)} copy-done((f32[256,1024]{1,0:T(8,128)}, f32[256,1024]{1,0:T(8,128)S(1)}, u32[]{:S(2)}) %copy-start.4) | copy-done | bytes 1048600
  33.0 11.5 %conditional.11 = (bf16[128,1024]{1,0:T(8,128)(2,1)}) conditional(s32[]{:T(128)} %bitcast.4, bf16[128,1024]{1,0:T(8,128)(2,1)S(1)} %get-tuple-element.228, bf16[128,1024]{1,0:T(8,128)(2,1)S(1)} %get-tuple-element.228, bf16[128,1024]{1,0:T(8,128)(2,1)S(1)} %get-tuple-element.228, ...), branch_computations={%region_39.40_spmd, %region_40.41_spmd, %region_41.42_spmd, %regio... | conditional | bytes 1048624 | solution.py:82
  33.0 1.3 %collective-permute-start.47 = (bf16[128,1024]{1,0:T(8,128)(2,1)S(1)}, bf16[128,1024]{1,0:T(8,128)(2,1)}, u32[]{:S(2)}, u32[]{:S(2)}) collective-permute-start(bf16[128,1024]{1,0:T(8,128)(2,1)S(1)} %param.55), channel_id=1, source_target_pairs={{1,30},{3,28},{5,26},{7,24},{9,22},{11,20},{13,18},{15,16},{17,14}... | collective-permute-start | bytes 786440 | tf_op jit(solution)/shard_map/cond/branch_15_fun/ppermute | solution.py:78
  34.3 10.2 %collective-permute-done.47 = bf16[128,1024]{1,0:T(8,128)(2,1)} collective-permute-done((bf16[128,1024]{1,0:T(8,128)(2,1)S(1)}, bf16[128,1024]{1,0:T(8,128)(2,1)}, u32[]{:S(2)}, u32[]{:S(2)}) %collective-permute-start.47) | collective-permute-done | bytes 262176 | tf_op jit(solution)/shard_map/cond/branch_15_fun/ppermute | solution.py:78
  44.5 7.8 %conditional.12 = (bf16[128,1024]{1,0:T(8,128)(2,1)}) conditional(s32[]{:T(128)} %bitcast.7, bf16[128,1024]{1,0:T(8,128)(2,1)S(1)} %get-tuple-element.227, bf16[128,1024]{1,0:T(8,128)(2,1)S(1)} %get-tuple-element.227, bf16[128,1024]{1,0:T(8,128)(2,1)S(1)} %get-tuple-element.227, ...), branch_computations={%region_55.56_spmd, %region_56.57_spmd, %region_57.58_spmd, %regio... | conditional | bytes 1048624 | solution.py:82
  44.5 1.3 %collective-permute-start.49 = (bf16[128,1024]{1,0:T(8,128)(2,1)S(1)}, bf16[128,1024]{1,0:T(8,128)(2,1)}, u32[]{:S(2)}, u32[]{:S(2)}) collective-permute-start(bf16[128,1024]{1,0:T(8,128)(2,1)S(1)} %param.57), channel_id=1, source_target_pairs={{1,2},{3,0},{5,6},{7,4},{9,10},{11,8},{13,14},{15,12},{17,18},{19,... | collective-permute-start | bytes 786440 | tf_op jit(solution)/shard_map/cond/branch_1_fun/ppermute | solution.py:78
  45.8 6.5 %collective-permute-done.49 = bf16[128,1024]{1,0:T(8,128)(2,1)} collective-permute-done((bf16[128,1024]{1,0:T(8,128)(2,1)S(1)}, bf16[128,1024]{1,0:T(8,128)(2,1)}, u32[]{:S(2)}, u32[]{:S(2)}) %collective-permute-start.49) | collective-permute-done | bytes 262176 | tf_op jit(solution)/shard_map/cond/branch_1_fun/ppermute | solution.py:78
  52.3 0.0 collective-permute-done.65
  52.3 1.4 %pad_maximum_fusion.1 = (bf16[256,1024]{1,0:T(8,128)(2,1)S(1)}, bf16[256,1024]{1,0:T(8,128)(2,1)S(1)}) fusion(bf16[128,1024]{1,0:T(8,128)(2,1)} %get-tuple-element.250, bf16[128,1024]{1,0:T(8,128)(2,1)} %get-tuple-element.249, bf16[256,1024]{1,0:T(8,128)(2,1)} %collective-permute-done.65, bf16[256,1024]{1,0:T(8,128)(2,1)S(1)} %broadcast_select_fusion.1, ...), kind=kLoop, calls=%fused_computation.44 | loop fusion | flops 1310720 | bytes 2621441 | tf_op jit(solution)/shard_map/concatenate | solution.py:242
  53.7 0.0 copy-start
  53.7 0.0 copy-start.1
  53.8 0.0 copy-start.2
  53.8 2.3 %conditional.13 = (f32[256,1024]{1,0:T(8,128)}) conditional(s32[]{:T(128)} %convert_element_type.39, f32[256,1024]{1,0:T(8,128)} %copy-done.4, (bf16[256,256]{1,0:T(8,128)(2,1)}, bf16[256,1024]{1,0:T(8,128)(2,1)S(1)}) %tuple.240), branch_computations={%region_71.72_spmd, %region_72.73_spmd} | conditional | flops 134479872 | bytes 1703944 | solution.py:244
  53.8 2.3 %convolution_multiply_fusion.7 = f32[256,1024]{1,0:T(8,128)} fusion(bf16[256,256]{1,0:T(8,128)(2,1)} %get-tuple-element.194, bf16[256,1024]{1,0:T(8,128)(2,1)S(1)} %get-tuple-element.195), kind=kOutput, calls=%fused_computation.42 | convolution fusion | flops 134479872 | bytes 1703936 | tf_op jit(solution)/shard_map/cond/branch_1_fun/dot_general | solution.py:36
  56.1 15.7 %outer.1 = (bf16[256,1024]{1,0:T(8,128)(2,1)S(1)}, bf16[256,1024]{1,0:T(8,128)(2,1)S(1)}) custom-call(s32[8,1024]{1,0:T(8,128)S(1)} %scatter.14.masks, f32[256,1024]{1,0:T(8,128)} %get-tuple-element.251.grad, bf16[256,1024]{1,0:T(8,128)(2,1)S(1)} %bitcast.27, bf16[256,1024]{1,0:T(8,128)(2,1)S(1)} %bitcast.28, bf16[256,1024]{1,0:T(8,128)(2,1)S(1)} %bitcast.39, ...), custom_call_target="tpu_custom_call" | custom-call | tf_op jit(solution)/shard_map/outer/pallas_call | solution.py:186
  71.8 0.8 %copy.90 = bf16[1,1,256,1024]{3,2,1,0:T(8,128)(2,1)} copy(bf16[1,1,256,1024]{3,2,1,0:T(8,128)(2,1)S(1)} %bitcast.31) | data formatting | bytes 1048576
  72.6 0.8 %copy.91 = bf16[1,1,256,1024]{3,2,1,0:T(8,128)(2,1)} copy(bf16[1,1,256,1024]{3,2,1,0:T(8,128)(2,1)S(1)} %bitcast.30) | data formatting | bytes 1048576
  (13 shorter events, 0.1 us)
Async XLA Ops:
  0.6 8.6 %copy-start.5 = (bf16[1,1,1024,256]{3,2,1,0:T(8,128)(2,1)S(1)}, bf16[1,1,1024,256]{3,2,1,0:T(8,128)(2,1)}, u32[]{:S(2)}) copy-start(bf16[1,1,1024,256]{3,2,1,0:T(8,128)(2,1)} %param.84) | copy-start | bytes 1572868
  0.6 1.3 %copy-start.3 = (bf16[1,1,256,1024]{3,2,1,0:T(8,128)(2,1)S(1)}, bf16[1,1,256,1024]{3,2,1,0:T(8,128)(2,1)}, u32[]{:S(2)}) copy-start(bf16[1,1,256,1024]{3,2,1,0:T(8,128)(2,1)} %param.86) | copy-start | bytes 1572868
  1.9 28.0 %collective-permute-start.64 = (bf16[256,1024]{1,0:T(8,128)(2,1)S(1)}, bf16[256,1024]{1,0:T(8,128)(2,1)S(1)}, u32[]{:S(2)}, u32[]{:S(2)}) collective-permute-start(bf16[256,1024]{1,0:T(8,128)(2,1)S(1)} %bitcast.36), channel_id=1, source_target_pairs={{0,2},{2,0},{4,6},{6,4},{8,10},{10,8},{12,14},{14,12},{16,18},{18,... | collective-permute-start | bytes 1572872 | tf_op jit(solution)/shard_map/ppermute | solution.py:12
  4.9 0.7 copy-start.8
  7.4 0.7 copy-start.9
  9.5 1.0 %copy-start.7 = (bf16[1024,256]{1,0:T(8,128)(2,1)S(1)}, bf16[1024,256]{1,0:T(8,128)(2,1)}, u32[]{:S(2)}) copy-start(bf16[1024,256]{1,0:T(8,128)(2,1)} %get-tuple-element.187) | copy-start | bytes 1572868 | tf_op jit(solution)/shard_map/cond
  12.8 6.7 %collective-permute-start.15 = (bf16[128,1024]{1,0:T(8,128)(2,1)S(1)}, bf16[128,1024]{1,0:T(8,128)(2,1)}, u32[]{:S(2)}, u32[]{:S(2)}) collective-permute-start(bf16[128,1024]{1,0:T(8,128)(2,1)S(1)} %param.21), channel_id=1, source_target_pairs={{0,31},{2,29},{4,27},{6,25},{8,23},{10,21},{12,19},{14,17},{16,15}... | collective-permute-start | bytes 786440 | tf_op jit(solution)/shard_map/cond/branch_15_fun/ppermute | solution.py:78
  19.6 10.3 %collective-permute-start.17 = (bf16[128,1024]{1,0:T(8,128)(2,1)S(1)}, bf16[128,1024]{1,0:T(8,128)(2,1)}, u32[]{:S(2)}, u32[]{:S(2)}) collective-permute-start(bf16[128,1024]{1,0:T(8,128)(2,1)S(1)} %param.23), channel_id=1, source_target_pairs={{0,3},{2,1},{4,7},{6,5},{8,11},{10,9},{12,15},{14,13},{16,19},{18,... | collective-permute-start | bytes 786440 | tf_op jit(solution)/shard_map/cond/branch_1_fun/ppermute | solution.py:78
  30.0 22.3 %collective-permute-start.65 = (bf16[256,1024]{1,0:T(8,128)(2,1)S(1)}, bf16[256,1024]{1,0:T(8,128)(2,1)}, u32[]{:S(2)}, u32[]{:S(2)}) collective-permute-start(bf16[256,1024]{1,0:T(8,128)(2,1)S(1)} %broadcast_select_fusion.1), channel_id=1, source_target_pairs={{0,4},{2,6},{4,0},{6,2},{8,12},{10,14},{12,8},{14,10},{16,20},{18,... | collective-permute-start | bytes 1572872 | tf_op jit(solution)/shard_map/ppermute | solution.py:12
  30.7 1.2 %copy-start.6 = (bf16[1,1,1024,256]{3,2,1,0:T(8,128)(2,1)S(1)}, bf16[1,1,1024,256]{3,2,1,0:T(8,128)(2,1)}, u32[]{:S(2)}) copy-start(bf16[1,1,1024,256]{3,2,1,0:T(8,128)(2,1)} %param.85) | copy-start | bytes 1572868
  32.0 1.0 %copy-start.4 = (f32[256,1024]{1,0:T(8,128)}, f32[256,1024]{1,0:T(8,128)S(1)}, u32[]{:S(2)}) copy-start(f32[256,1024]{1,0:T(8,128)S(1)} %get-tuple-element.213) | copy-start | bytes 3145732
  33.0 11.5 %collective-permute-start.47 = (bf16[128,1024]{1,0:T(8,128)(2,1)S(1)}, bf16[128,1024]{1,0:T(8,128)(2,1)}, u32[]{:S(2)}, u32[]{:S(2)}) collective-permute-start(bf16[128,1024]{1,0:T(8,128)(2,1)S(1)} %param.55), channel_id=1, source_target_pairs={{1,30},{3,28},{5,26},{7,24},{9,22},{11,20},{13,18},{15,16},{17,14}... | collective-permute-start | bytes 786440 | tf_op jit(solution)/shard_map/cond/branch_15_fun/ppermute | solution.py:78
  44.5 7.8 %collective-permute-start.49 = (bf16[128,1024]{1,0:T(8,128)(2,1)S(1)}, bf16[128,1024]{1,0:T(8,128)(2,1)}, u32[]{:S(2)}, u32[]{:S(2)}) collective-permute-start(bf16[128,1024]{1,0:T(8,128)(2,1)S(1)} %param.57), channel_id=1, source_target_pairs={{1,2},{3,0},{5,6},{7,4},{9,10},{11,8},{13,14},{15,12},{17,18},{19,... | collective-permute-start | bytes 786440 | tf_op jit(solution)/shard_map/cond/branch_1_fun/ppermute | solution.py:78
  53.7 2.4 %copy-start = (bf16[1,1,256,1024]{3,2,1,0:T(8,128)(2,1)S(1)}, bf16[1,1,256,1024]{3,2,1,0:T(8,128)(2,1)}, u32[]{:S(2)}) copy-start(bf16[1,1,256,1024]{3,2,1,0:T(8,128)(2,1)} %param.87) | copy-start | bytes 1572868
  53.7 2.4 %copy-start.1 = (bf16[1,1,256,1024]{3,2,1,0:T(8,128)(2,1)S(1)}, bf16[1,1,256,1024]{3,2,1,0:T(8,128)(2,1)}, u32[]{:S(2)}) copy-start(bf16[1,1,256,1024]{3,2,1,0:T(8,128)(2,1)} %param.88) | copy-start | bytes 1572868
  53.8 2.4 %copy-start.2 = (bf16[1,1,256,1024]{3,2,1,0:T(8,128)(2,1)S(1)}, bf16[1,1,256,1024]{3,2,1,0:T(8,128)(2,1)}, u32[]{:S(2)}) copy-start(bf16[1,1,256,1024]{3,2,1,0:T(8,128)(2,1)} %param.89) | copy-start | bytes 1572868

commit v2 on v1

--- a/solution.py
+++ b/solution.py
@@ -59,25 +59,55 @@
     return (grad_term, back_rows.astype(jnp.bfloat16))
 
 
+def hop_kernel(flip, source, target, rows, out, send_sem, recv_sem):
+    me, section = lax.axis_index("rep"), lax.axis_index("section")
+    peer = me
+    for bit in range(flip.bit_length()):
+        if flip >> bit & 1:
+            peer = peer + (1 << bit) - (2 << bit) * ((me // (1 << bit)) % 2)
+    other = {"rep": peer, "section": section if source == target else 1 - section}
+    barrier = pltpu.get_barrier_semaphore()
+    pl.semaphore_signal(barrier, inc=1, device_id=other, device_id_type=pl.DeviceIdType.MESH)
+    pl.semaphore_wait(barrier, 1)
+    copy = pltpu.make_async_remote_copy(
+        src_ref=rows, dst_ref=out, send_sem=send_sem, recv_sem=recv_sem,
+        device_id=other, device_id_type=pl.DeviceIdType.MESH,
+    )
+
+    @pl.when(section == source)
+    def _():
+        copy.start()
+        copy.wait_send()
+
+    @pl.when(section == target)
+    def _():
+        copy.wait_recv()
+
+
 def send_rows(payload, flip_key, source):
-    replicas = lax.axis_size("rep")
-    bits = replicas.bit_length() - 1
+    bits = lax.axis_size("rep").bit_length() - 1
     starts = list(range(0, bits, 4))
-    for start in starts:
+    for index, start in enumerate(starts):
         width = min(4, bits - start)
         target = 1 - source if start == starts[-1] else source
 
-        def branch(flip, start=start, target=target):
-            pairs = [
-                (2 * r + source, 2 * (r ^ flip << start) + target) for r in range(replicas)
-            ]
-
-            def run(rows):
-                if target == source and flip == 0:
-                    return rows
-                return lax.ppermute(rows, ("rep", "section"), pairs)
-
-            return run
+        def branch(flip, index=index, start=start, target=target):
+            if target == source and flip == 0:
+                return lambda rows: rows
+            in_vmem = pl.BlockSpec(memory_space=pltpu.VMEM)
+            return pl.pallas_call(
+                functools.partial(hop_kernel, flip << start, source, target),
+                out_shape=jax.ShapeDtypeStruct(payload.shape, payload.dtype),
+                in_specs=[in_vmem],
+                out_specs=in_vmem,
+                scratch_shapes=[pltpu.SemaphoreType.DMA, pltpu.SemaphoreType.DMA],
+                compiler_params=pltpu.CompilerParams(
+                    collective_id=1 + (index * 2 + source) * 16 + flip,
+                    has_side_effects=True,
+                    vmem_limit_bytes=4 * 1024 * 1024,
+                ),
+                name="hop",
+            )
 
         payload = lax.switch(
             flip_key >> start & (1 << width) - 1, [branch(f) for f in range(1 << width)], payload

time: 74.1 us -> 67.2 us (0.907)
  Pallas kernels: 15.7 us -> 44.9 us
  waiting for transfers between devices: 23.1 us -> 0.01 us
  starting transfers between devices: 16.8 us -> 3.54 us
  other arithmetic: 2.81 us -> 1.59 us
  local copies, waits for them, and re-layouts: 7.32 us -> 8.25 us
    pallas_call x0 -> x4, Pallas kernels: none -> 29.2 us  [send_rows(): lax.switch(flip_key >> start & (1 << width) - 1, [branch(f) for f in rang...]
    ppermute x4 -> x0, waiting for transfers between devices: 23.1 us -> none  [run(): return lax.ppermute(rows, ('rep', 'section'), pairs)]
    ppermute x4 -> x0, starting transfers between devices: 13.2 us -> none  [run(): return lax.ppermute(rows, ('rep', 'section'), pairs)]
    concatenate x1, other arithmetic: 1.12 us -> 0.04 us  [on_device(): arrived = jnp.concatenate(arrived)]
    unnamed x21, local copies, waits for them, and re-layouts: 5.19 us -> 6.12 us
  transfers between devices with their start and end apart: 6 -> 2, of which waited for: 4 -> 0; matrix products, arithmetic and copies ran while one was open for 7% -> 6% of each run, Pallas kernels for 0% -> 44%
where the time goes in v2:
time: 67.2 us; the launch traced here: 66.2 us
  Pallas kernels  44.9 us (67%)
  local copies, waits for them, and re-layouts  8.25 us (12%)
  matrix products  4.9 us (7%)
  starting transfers between devices  3.54 us (5%)
  between operations  2.79 us (4%)
  other arithmetic  1.59 us (2%)
    pallas_call x4, Pallas kernels, send_rows(): lax.switch(flip_key >> start & (1 << width) - 1, [branch(f) for f in rang...  29.2 us
    pallas_call x1, Pallas kernels, outer_update(): pl.pallas_call(functools.partial(outer_kernel, chunks), out_shape=(out, o...  15.7 us
    unnamed x21, local copies, waits for them, and re-layouts  6.12 us
    ppermute x2, starting transfers between devices, partner_2(): lax.ppermute(x, axis, [(i, i ^ 1 << bit) for i in range(lax.axis_size(axi...  3.54 us
    dot_general x1, matrix products, grad_rows(): lax.dot_general(hidden, cotangent, (((0,), (0,)), ((), ())), preferred_el...  2.33 us
  transfers between devices with their start and end apart: 2, of which 0 were waited for; matrix products, arithmetic and copies ran while one was open for 6% of the time, Pallas kernels for 44%

profile of v2, /device:TPU:0, one launch (start us, length us, event | category | flops | bytes accessed | tf_op | source)
XLA Modules:
  0.0 66.2 jit_solution(10923584863159486876)
XLA Ops:
  0.6 0.0 copy-start.5
  0.6 0.0 copy-start.3
  0.6 1.1 %copy.89 = bf16[1,1,2,128,1024]{4,3,2,1,0:T(8,128)(2,1)S(1)} copy(bf16[1,1,2,128,1024]{4,3,2,1,0:T(8,128)(2,1)} %param.83) | data formatting | bytes 1048576
  1.8 0.1 copy-done.3
  1.9 3.0 %collective-permute-start = (bf16[256,1024]{1,0:T(8,128)(2,1)S(1)}, bf16[256,1024]{1,0:T(8,128)(2,1)S(1)}, u32[]{:S(2)}, u32[]{:S(2)}) collective-permute-start(bf16[256,1024]{1,0:T(8,128)(2,1)S(1)} %bitcast.36), channel_id=1, source_target_pairs={{0,2},{2,0},{4,6},{6,4},{8,10},{10,8},{12,14},{14,12},{16,18},{18,... | collective-permute-start | bytes 1572872 | tf_op jit(solution)/shard_map/ppermute | solution.py:12
  4.9 0.7 %copy-done.8 = s32[2,16]{1,0:T(2,128)S(1)} copy-done((s32[2,16]{1,0:T(2,128)S(1)}, s32[2,16]{1,0:T(2,128)}, u32[]{:S(2)}) %copy-start.8) | copy-done | bytes 152
  5.5 0.5 fusion.24
  7.4 0.0 copy-start.9
  7.4 0.6 copy-done.9
  8.0 0.6 dynamic_slice.3
  9.3 0.0 copy-done.5
  9.3 3.5 %conditional.7 = (bf16[256,1024]{1,0:T(8,128)(2,1)S(1)}, bf16[256,256]{1,0:T(8,128)(2,1)}) conditional(s32[]{:T(128)} %convert_element_type.39, bf16[256,1024]{1,0:T(8,128)(2,1)S(1)} %bitcast.32, (bf16[256,1024]{1,0:T(8,128)(2,1)S(1)}, bf16[1024,256]{1,0:T(8,128)(2,1)S(1)}, bf16[1024,256]{1,0:T(8,128)(2,1)}, bf16[256,1024]{1,0:T(8,128)(2,1)S(1)}) %tuple.327), branch_computations={%region_0.0_spmd, %region_1.3_spmd} | conditional | flops 406585600 | bytes 7083052 | solution.py:252
  9.3 0.2 fusion.3
  9.5 0.0 copy-start.7
  9.5 0.3 convolution_multiply_fusion.2
  9.9 0.7 %copy-done.7 = bf16[1024,256]{1,0:T(8,128)(2,1)S(1)} copy-done((bf16[1024,256]{1,0:T(8,128)(2,1)S(1)}, bf16[1024,256]{1,0:T(8,128)(2,1)}, u32[]{:S(2)}) %copy-start.7) | copy-done | bytes 524312 | tf_op jit(solution)/shard_map/cond
  10.5 1.0 %fusion.2 = bf16[256,256]{1,0:T(8,128)(2,1)} fusion(bf16[1024,256]{1,0:T(8,128)(2,1)S(1)} %copy-done.7, f32[256,256]{1,0:T(8,128)S(1)} %convolution_multiply_fusion.2, bf16[256,1024]{1,0:T(8,128)(2,1)S(1)} %get-tuple-element.185, f32[256]{0:T(256)S(1)} %add_rsqrt_fusion), kind=kOutput, calls=%fused_computation.8 | convolution fusion | flops 135462912 | bytes 1442816 | tf_op jit(solution)/shard_map/cond/branch_1_fun/dot_general | solution.py:22
  11.5 1.2 %fusion = bf16[256,1024]{1,0:T(8,128)(2,1)S(1)} fusion(bf16[256,256]{1,0:T(8,128)(2,1)} %fusion.2, bf16[256,1024]{1,0:T(8,128)(2,1)S(1)} %get-tuple-element.188, bf16[256,1024]{1,0:T(8,128)(2,1)S(1)} %get-tuple-element.185), kind=kOutput, calls=%fused_computation.4 | convolution fusion | flops 135266304 | bytes 1703936 | tf_op jit(solution)/shard_map/cond/branch_1_fun/dot_general | solution.py:24
  12.8 5.0 %conditional.8 = (bf16[128,1024]{1,0:T(8,128)(2,1)S(1)}) conditional(s32[]{:T(128)} %bitcast.4, bf16[128,1024]{1,0:T(8,128)(2,1)S(1)} %get-tuple-element.230, bf16[128,1024]{1,0:T(8,128)(2,1)S(1)} %get-tuple-element.230, bf16[128,1024]{1,0:T(8,128)(2,1)S(1)} %get-tuple-element.230, ...), branch_computations={%region_3.4_spmd, %region_4.5_spmd, %region_5.6_spmd, %region_6.7_... | conditional | bytes 8 | solution.py:112
  12.9 4.9 %hop.79 = bf16[128,1024]{1,0:T(8,128)(2,1)S(1)} custom-call(bf16[128,1024]{1,0:T(8,128)(2,1)S(1)} %rows.15), custom_call_target="tpu_custom_call" | custom-call | tf_op jit(solution)/shard_map/cond/branch_15_fun/hop/pallas_call | solution.py:112
  17.8 9.0 %conditional.9 = (bf16[128,1024]{1,0:T(8,128)(2,1)S(1)}) conditional(s32[]{:T(128)} %bitcast.7, bf16[128,1024]{1,0:T(8,128)(2,1)S(1)} %get-tuple-element.229, bf16[128,1024]{1,0:T(8,128)(2,1)S(1)} %get-tuple-element.229, bf16[128,1024]{1,0:T(8,128)(2,1)S(1)} %get-tuple-element.229, ...), branch_computations={%region_19.20_spmd, %region_20.21_spmd, %region_21.22_spmd, %regio... | conditional | bytes 8 | solution.py:112
  17.8 9.0 %hop.81 = bf16[128,1024]{1,0:T(8,128)(2,1)S(1)} custom-call(bf16[128,1024]{1,0:T(8,128)(2,1)S(1)} %rows.17), custom_call_target="tpu_custom_call" | custom-call | tf_op jit(solution)/shard_map/cond/branch_1_fun/hop/pallas_call | solution.py:112
  26.8 0.0 collective-permute-done
  26.8 0.1 broadcast_select_fusion.1
  26.9 0.6 collective-permute-start.1
  27.5 0.1 scatter.13
  27.6 0.1 scatter.14.masks
  27.6 0.0 copy-start.6
  27.7 1.0 %copy-done.6 = bf16[1,1,1024,256]{3,2,1,0:T(8,128)(2,1)S(1)} copy-done((bf16[1,1,1024,256]{3,2,1,0:T(8,128)(2,1)S(1)}, bf16[1,1,1024,256]{3,2,1,0:T(8,128)(2,1)}, u32[]{:S(2)}) %copy-start.6) | copy-done | bytes 524312
  28.7 0.1 conditional.10
  28.7 0.1 broadcast.117
  28.9 0.9 %copy-done.4 = f32[256,1024]{1,0:T(8,128)} copy-done((f32[256,1024]{1,0:T(8,128)}, f32[256,1024]{1,0:T(8,128)S(1)}, u32[]{:S(2)}) %copy-start.4) | copy-done | bytes 1048600
  29.8 9.5 %conditional.11 = (bf16[128,1024]{1,0:T(8,128)(2,1)S(1)}) conditional(s32[]{:T(128)} %bitcast.4, bf16[128,1024]{1,0:T(8,128)(2,1)S(1)} %get-tuple-element.228, bf16[128,1024]{1,0:T(8,128)(2,1)S(1)} %get-tuple-element.228, bf16[128,1024]{1,0:T(8,128)(2,1)S(1)} %get-tuple-element.228, ...), branch_computations={%region_39.40_spmd, %region_40.41_spmd, %region_41.42_spmd, %regio... | conditional | bytes 8 | solution.py:112
  29.8 9.5 %hop.111 = bf16[128,1024]{1,0:T(8,128)(2,1)S(1)} custom-call(bf16[128,1024]{1,0:T(8,128)(2,1)S(1)} %rows.47), custom_call_target="tpu_custom_call" | custom-call | tf_op jit(solution)/shard_map/cond/branch_15_fun/hop/pallas_call | solution.py:112
  39.3 5.9 %conditional.12 = (bf16[128,1024]{1,0:T(8,128)(2,1)S(1)}) conditional(s32[]{:T(128)} %bitcast.7, bf16[128,1024]{1,0:T(8,128)(2,1)S(1)} %get-tuple-element.227, bf16[128,1024]{1,0:T(8,128)(2,1)S(1)} %get-tuple-element.227, bf16[128,1024]{1,0:T(8,128)(2,1)S(1)} %get-tuple-element.227, ...), branch_computations={%region_55.56_spmd, %region_56.57_spmd, %region_57.58_spmd, %regio... | conditional | bytes 8 | solution.py:112
  39.4 5.8 %hop.113 = bf16[128,1024]{1,0:T(8,128)(2,1)S(1)} custom-call(bf16[128,1024]{1,0:T(8,128)(2,1)S(1)} %rows.49), custom_call_target="tpu_custom_call" | custom-call | tf_op jit(solution)/shard_map/cond/branch_1_fun/hop/pallas_call | solution.py:112
  45.2 0.0 collective-permute-done.1
  45.2 1.3 %pad_maximum_fusion.1 = (bf16[256,1024]{1,0:T(8,128)(2,1)S(1)}, bf16[256,1024]{1,0:T(8,128)(2,1)S(1)}) fusion(bf16[128,1024]{1,0:T(8,128)(2,1)S(1)} %get-tuple-element.250, bf16[128,1024]{1,0:T(8,128)(2,1)S(1)} %get-tuple-element.249, bf16[256,1024]{1,0:T(8,128)(2,1)} %collective-permute-done.1, bf16[256,1024]{1,0:T(8,128)(2,1)S(1)} %broadcast_select_fusion.1, ...), kind=kLoop, calls=%fused_computation.44 | loop fusion | flops 1310720 | bytes 2621441 | tf_op jit(solution)/shard_map/concatenate | solution.py:272
  46.5 0.0 copy-start
  46.6 0.0 copy-start.1
  46.6 0.0 copy-start.2
  46.6 2.3 %conditional.13 = (f32[256,1024]{1,0:T(8,128)}) conditional(s32[]{:T(128)} %convert_element_type.39, f32[256,1024]{1,0:T(8,128)} %copy-done.4, (bf16[256,256]{1,0:T(8,128)(2,1)}, bf16[256,1024]{1,0:T(8,128)(2,1)S(1)}) %tuple.240), branch_computations={%region_71.72_spmd, %region_72.73_spmd} | conditional | flops 134479872 | bytes 1703944 | solution.py:274
  46.6 2.3 %convolution_multiply_fusion.7 = f32[256,1024]{1,0:T(8,128)} fusion(bf16[256,256]{1,0:T(8,128)(2,1)} %get-tuple-element.194, bf16[256,1024]{1,0:T(8,128)(2,1)S(1)} %get-tuple-element.195), kind=kOutput, calls=%fused_computation.42 | convolution fusion | flops 134479872 | bytes 1703936 | tf_op jit(solution)/shard_map/cond/branch_1_fun/dot_general | solution.py:36
  48.9 0.0 copy-done
  48.9 0.0 copy-done.2
  48.9 15.7 %outer.1 = (bf16[256,1024]{1,0:T(8,128)(2,1)S(1)}, bf16[256,1024]{1,0:T(8,128)(2,1)S(1)}) custom-call(s32[8,1024]{1,0:T(8,128)S(1)} %scatter.14.masks, f32[256,1024]{1,0:T(8,128)} %get-tuple-element.251.grad, bf16[256,1024]{1,0:T(8,128)(2,1)S(1)} %bitcast.27, bf16[256,1024]{1,0:T(8,128)(2,1)S(1)} %bitcast.28, bf16[256,1024]{1,0:T(8,128)(2,1)S(1)} %bitcast.39, ...), custom_call_target="tpu_custom_call" | custom-call | tf_op jit(solution)/shard_map/outer/pallas_call | solution.py:216
  64.6 0.8 %copy.90 = bf16[1,1,256,1024]{3,2,1,0:T(8,128)(2,1)} copy(bf16[1,1,256,1024]{3,2,1,0:T(8,128)(2,1)S(1)} %bitcast.31) | data formatting | bytes 1048576
  65.4 0.8 %copy.91 = bf16[1,1,256,1024]{3,2,1,0:T(8,128)(2,1)} copy(bf16[1,1,256,1024]{3,2,1,0:T(8,128)(2,1)S(1)} %bitcast.30) | data formatting | bytes 1048576
  (9 shorter events, 0.1 us)
Async XLA Ops:
  0.6 8.6 %copy-start.5 = (bf16[1,1,1024,256]{3,2,1,0:T(8,128)(2,1)S(1)}, bf16[1,1,1024,256]{3,2,1,0:T(8,128)(2,1)}, u32[]{:S(2)}) copy-start(bf16[1,1,1024,256]{3,2,1,0:T(8,128)(2,1)} %param.84) | copy-start | bytes 1572868
  0.6 1.3 %copy-start.3 = (bf16[1,1,256,1024]{3,2,1,0:T(8,128)(2,1)S(1)}, bf16[1,1,256,1024]{3,2,1,0:T(8,128)(2,1)}, u32[]{:S(2)}) copy-start(bf16[1,1,256,1024]{3,2,1,0:T(8,128)(2,1)} %param.86) | copy-start | bytes 1572868
  1.9 24.9 %collective-permute-start = (bf16[256,1024]{1,0:T(8,128)(2,1)S(1)}, bf16[256,1024]{1,0:T(8,128)(2,1)S(1)}, u32[]{:S(2)}, u32[]{:S(2)}) collective-permute-start(bf16[256,1024]{1,0:T(8,128)(2,1)S(1)} %bitcast.36), channel_id=1, source_target_pairs={{0,2},{2,0},{4,6},{6,4},{8,10},{10,8},{12,14},{14,12},{16,18},{18,... | collective-permute-start | bytes 1572872 | tf_op jit(solution)/shard_map/ppermute | solution.py:12
  4.9 0.7 %copy-start.8 = (s32[2,16]{1,0:T(2,128)S(1)}, s32[2,16]{1,0:T(2,128)}, u32[]{:S(2)}) copy-start(s32[2,16]{1,0:T(2,128)} %param.90) | copy-start | bytes 388
  7.4 0.7 copy-start.9
  9.5 1.0 %copy-start.7 = (bf16[1024,256]{1,0:T(8,128)(2,1)S(1)}, bf16[1024,256]{1,0:T(8,128)(2,1)}, u32[]{:S(2)}) copy-start(bf16[1024,256]{1,0:T(8,128)(2,1)} %get-tuple-element.187) | copy-start | bytes 1572868 | tf_op jit(solution)/shard_map/cond
  26.9 18.3 %collective-permute-start.1 = (bf16[256,1024]{1,0:T(8,128)(2,1)S(1)}, bf16[256,1024]{1,0:T(8,128)(2,1)}, u32[]{:S(2)}, u32[]{:S(2)}) collective-permute-start(bf16[256,1024]{1,0:T(8,128)(2,1)S(1)} %broadcast_select_fusion.1), channel_id=1, source_target_pairs={{0,4},{2,6},{4,0},{6,2},{8,12},{10,14},{12,8},{14,10},{16,20},{18,... | collective-permute-start | bytes 1572872 | tf_op jit(solution)/shard_map/ppermute | solution.py:12
  27.6 1.0 %copy-start.6 = (bf16[1,1,1024,256]{3,2,1,0:T(8,128)(2,1)S(1)}, bf16[1,1,1024,256]{3,2,1,0:T(8,128)(2,1)}, u32[]{:S(2)}) copy-start(bf16[1,1,1024,256]{3,2,1,0:T(8,128)(2,1)} %param.85) | copy-start | bytes 1572868
  28.8 1.0 %copy-start.4 = (f32[256,1024]{1,0:T(8,128)}, f32[256,1024]{1,0:T(8,128)S(1)}, u32[]{:S(2)}) copy-start(f32[256,1024]{1,0:T(8,128)S(1)} %get-tuple-element.213) | copy-start | bytes 3145732
  46.5 2.4 %copy-start = (bf16[1,1,256,1024]{3,2,1,0:T(8,128)(2,1)S(1)}, bf16[1,1,256,1024]{3,2,1,0:T(8,128)(2,1)}, u32[]{:S(2)}) copy-start(bf16[1,1,256,1024]{3,2,1,0:T(8,128)(2,1)} %param.87) | copy-start | bytes 1572868
  46.6 2.4 %copy-start.1 = (bf16[1,1,256,1024]{3,2,1,0:T(8,128)(2,1)S(1)}, bf16[1,1,256,1024]{3,2,1,0:T(8,128)(2,1)}, u32[]{:S(2)}) copy-start(bf16[1,1,256,1024]{3,2,1,0:T(8,128)(2,1)} %param.88) | copy-start | bytes 1572868
  46.6 2.4 %copy-start.2 = (bf16[1,1,256,1024]{3,2,1,0:T(8,128)(2,1)S(1)}, bf16[1,1,256,1024]{3,2,1,0:T(8,128)(2,1)}, u32[]{:S(2)}) copy-start(bf16[1,1,256,1024]{3,2,1,0:T(8,128)(2,1)} %param.89) | copy-start | bytes 1572868

commit v3 on v2

--- a/solution.py
+++ b/solution.py
@@ -113,6 +113,74 @@
             flip_key >> start & (1 << width) - 1, [branch(f) for f in range(1 << width)], payload
         )
     return payload
+
+
+def twin_kernel(flips, source, rows, out, send_sem, recv_sem):
+    me, section = lax.axis_index("rep"), lax.axis_index("section")
+    others = []
+    for flip in flips:
+        peer = me
+        for bit in range(flip.bit_length()):
+            if flip >> bit & 1:
+                peer = peer + (1 << bit) - (2 << bit) * ((me // (1 << bit)) % 2)
+        others.append({"rep": peer, "section": 1 - section})
+    barrier = pltpu.get_barrier_semaphore()
+    for other in others:
+        pl.semaphore_signal(barrier, inc=1, device_id=other, device_id_type=pl.DeviceIdType.MESH)
+    pl.semaphore_wait(barrier, 2)
+    copies = [
+        pltpu.make_async_remote_copy(
+            src_ref=rows.at[b], dst_ref=out.at[b], send_sem=send_sem.at[b],
+            recv_sem=recv_sem.at[b], device_id=others[b],
+            device_id_type=pl.DeviceIdType.MESH,
+        )
+        for b in range(2)
+    ]
+
+    @pl.when(section == source)
+    def _():
+        for copy in copies:
+            copy.start()
+        for copy in copies:
+            copy.wait_send()
+
+    @pl.when(section != source)
+    def _():
+        for copy in copies:
+            copy.wait_recv()
+
+
+def send_batches(payload, flip_keys, source):
+    replicas = lax.axis_size("rep")
+    if payload.shape[0] != 2 or replicas > 16:
+        return jnp.stack(
+            [send_rows(payload[b], flip_keys[b], source) for b in range(payload.shape[0])]
+        )
+    in_vmem = pl.BlockSpec(memory_space=pltpu.VMEM)
+    span = replicas - 1
+
+    flips = [(low + 1, high + 1) for high in range(span) for low in range(high + 1)]
+
+    def branch(index):
+        return pl.pallas_call(
+            functools.partial(twin_kernel, flips[index], source),
+            out_shape=jax.ShapeDtypeStruct(payload.shape, payload.dtype),
+            in_specs=[in_vmem],
+            out_specs=in_vmem,
+            scratch_shapes=[pltpu.SemaphoreType.DMA((2,)), pltpu.SemaphoreType.DMA((2,))],
+            compiler_params=pltpu.CompilerParams(
+                collective_id=1 + source * len(flips) + index,
+                has_side_effects=True,
+                vmem_limit_bytes=4 * 1024 * 1024,
+            ),
+            name="twin",
+        )
+
+    return lax.switch(
+        flip_keys[1] * (flip_keys[1] - 1) // 2 + flip_keys[0] - 1,
+        [branch(index) for index in range(len(flips))],
+        payload,
+    )
 
 
 def outer_kernel(
@@ -228,14 +296,18 @@
 
 def on_device(ends, w_gate, w_up, slow_down, adam_m, adam_v, momentum, routes, partner):
     micro_count, row_count, model_width = ends.shape[2:]
-    own_data = ends.reshape(micro_count * row_count, model_width)
+    flip_keys = routes[:, 0]
+    own_data = ends[0, 0]
+    if micro_count == 2:
+        own_data = jnp.where(flip_keys[0] > flip_keys[1], own_data[::-1], own_data)
+        flip_keys = jnp.stack([jnp.min(flip_keys), jnp.max(flip_keys)])
+    own_data = own_data.reshape(micro_count * row_count, model_width)
     gate_w = w_gate[0, 0]
     up_w = w_up[0, 0]
     down_w = slow_down[0, 0]
     hidden_units = gate_w.shape[1]
     replica = lax.axis_index("rep")
     on_first = lax.axis_index("section") == 0
-    flip_keys = routes[:, 0]
     flip_bits = jnp.bitwise_xor(partner[replica], replica)
     near_slow = partner_2(down_w, "rep", 0)
 
@@ -251,9 +323,9 @@
 
     sent, hidden = lax.cond(on_first, first_forward, first_idle)
     sent = cut(sent)
-    arrived = [send_rows(sent[b], flip_keys[b], 0) for b in range(micro_count)]
-    near_slow, *arrived = lax.optimization_barrier((near_slow, *arrived))
-    arrived = jnp.concatenate(arrived)
+    arrived = send_batches(sent, flip_keys, 0)
+    near_slow, arrived = lax.optimization_barrier((near_slow, arrived))
+    arrived = arrived.reshape(own_data.shape)
     chosen_slow = jnp.where(flip_bits & 1 == 1, near_slow, down_w)
     far_slow = partner_2(chosen_slow, "rep", 1)
 
@@ -267,9 +339,9 @@
 
     last_term, back = lax.cond(on_first, last_idle, last_work)
     back = cut(back)
-    returned = [send_rows(back[b], flip_keys[b], 1) for b in range(micro_count)]
-    far_slow, *returned = lax.optimization_barrier((far_slow, *returned))
-    returned = jnp.concatenate(returned)
+    returned = send_batches(back, flip_keys, 1)
+    far_slow, returned = lax.optimization_barrier((far_slow, returned))
+    returned = returned.reshape(own_data.shape)
     partner_slow = jnp.where(flip_bits >> 1 & 1 == 1, far_slow, chosen_slow)
     grad_sum = lax.cond(
         on_first, lambda: grad_rows(returned, hidden, hidden_units), lambda: last_term

time: 67.2 us -> 74.2 us (1.10)
  Pallas kernels: 44.9 us -> 50.3 us
  other arithmetic: 1.59 us -> 4.57 us
  local copies, waits for them, and re-layouts: 8.25 us -> 5.35 us
  between operations: 2.79 us -> 4.67 us
    pallas_call x4 -> x2, Pallas kernels: 29.2 us -> 35 us  [send_batches(): lax.switch(flip_keys[1] * (flip_keys[1] - 1) // 2 + flip_keys[0] - 1, [br...]
    unnamed x21 -> x20, local copies, waits for them, and re-layouts: 6.12 us -> 3.25 us
    select_n x0 -> x2, other arithmetic: none -> 2.58 us  [the longest x1 1.48 us: on_device(): own_data = jnp.where(flip_keys[0] > flip_keys[1], own_data[::-1], own_data)]
    concatenate x2 -> x0, other arithmetic: 1.34 us -> none  [the longest x1 1.3 us: on_device(): returned = jnp.concatenate(returned)]
    select_n x1, other arithmetic: 0.06 us -> 1.16 us  [on_device(): chosen_slow = jnp.where(flip_bits & 1 == 1, near_slow, down_w)]
  transfers between devices with their start and end apart: 2 -> 2, of which waited for: 0 -> 0; matrix products, arithmetic and copies ran while one was open for 6% -> 9% of each run, Pallas kernels for 44% -> 47%
where the time goes in v3:
time: 74.2 us; the launch traced here: 73.8 us
  Pallas kernels  50.3 us (68%)
  local copies, waits for them, and re-layouts  5.35 us (7%)
  matrix products  4.88 us (7%)
  between operations  4.67 us (6%)
  other arithmetic  4.57 us (6%)
  starting transfers between devices  3.64 us (5%)
    pallas_call x2, Pallas kernels, send_batches(): lax.switch(flip_keys[1] * (flip_keys[1] - 1) // 2 + flip_keys[0] - 1, [br...  35 us
    pallas_call x1, Pallas kernels, outer_update(): pl.pallas_call(functools.partial(outer_kernel, chunks), out_shape=(out, o...  15.3 us
    ppermute x2, starting transfers between devices, partner_2(): lax.ppermute(x, axis, [(i, i ^ 1 << bit) for i in range(lax.axis_size(axi...  3.64 us
    unnamed x20, local copies, waits for them, and re-layouts  3.25 us
    dot_general x1, matrix products, grad_rows(): lax.dot_general(hidden, cotangent, (((0,), (0,)), ((), ())), preferred_el...  2.31 us
  transfers between devices with their start and end apart: 2, of which 0 were waited for; matrix products, arithmetic and copies ran while one was open for 9% of the time, Pallas kernels for 47%

profile of v3, /device:TPU:0, one launch (start us, length us, event | category | flops | bytes accessed | tf_op | source)
XLA Modules:
  0.0 73.8 jit_solution(10861925610401007220)
XLA Ops:
  0.6 0.0 copy-start.8
  0.6 3.0 %collective-permute-start = (bf16[256,1024]{1,0:T(8,128)(2,1)}, bf16[256,1024]{1,0:T(8,128)(2,1)}, u32[]{:S(2)}, u32[]{:S(2)}) collective-permute-start(bf16[256,1024]{1,0:T(8,128)(2,1)} %bitcast.184), channel_id=1, source_target_pairs={{0,2},{2,0},{4,6},{6,4},{8,10},{10,8},{12,14},{14,12},{16,18},{18,... | collective-permute-start | bytes 1572872 | tf_op jit(solution)/shard_map/ppermute | solution.py:12
  3.7 0.0 copy-done.8
  3.7 0.6 slice_reduce_fusion
  6.3 0.0 copy-start.9
  6.3 0.6 copy-done.9
  6.9 0.6 dynamic_slice.3
  8.2 0.5 fusion.20
  9.9 0.0 copy-start.3
  9.9 0.0 copy-start.5
  10.0 1.5 %reverse_select_fusion = bf16[2,128,1024]{2,1,0:T(8,128)(2,1)S(1)} fusion(bf16[2,128,1024]{2,1,0:T(8,128)(2,1)} %bitcast.193, pred[]{:T(512)} %bitcast.8), kind=kLoop, calls=%fused_computation.43 | loop fusion | flops 262144 | bytes 1048577 | tf_op jit(solution)/shard_map/jit(_where)/select_n | solution.py:302
  11.4 0.0 copy-done.3
  11.5 0.0 copy-done.5
  11.5 3.5 %conditional.5 = (bf16[256,1024]{1,0:T(8,128)(2,1)S(1)}, bf16[256,256]{1,0:T(8,128)(2,1)}) conditional(s32[]{:T(128)} %convert_element_type.45, bf16[256,1024]{1,0:T(8,128)(2,1)S(1)} %bitcast.179, (bf16[256,1024]{1,0:T(8,128)(2,1)S(1)}, bf16[1024,256]{1,0:T(8,128)(2,1)S(1)}, bf16[1024,256]{1,0:T(8,128)(2,1)}, bf16[256,1024]{1,0:T(8,128)(2,1)S(1)}) %tuple.1033), branch_computations={%region_2.3_spmd, %region_3.5_spmd} | conditional | flops 406585600 | bytes 7083052 | solution.py:324
  11.5 0.2 fusion.3
  11.7 0.0 copy-start.7
  11.7 0.3 convolution_multiply_fusion.2
  12.0 0.7 copy-done.7
  12.7 1.0 %fusion.2 = bf16[256,256]{1,0:T(8,128)(2,1)} fusion(bf16[1024,256]{1,0:T(8,128)(2,1)S(1)} %copy-done.7, f32[256,256]{1,0:T(8,128)S(1)} %convolution_multiply_fusion.2, bf16[256,1024]{1,0:T(8,128)(2,1)S(1)} %get-tuple-element.538, f32[256]{0:T(256)S(1)} %add_rsqrt_fusion), kind=kOutput, calls=%fused_computation.8 | convolution fusion | flops 135462912 | bytes 1442816 | tf_op jit(solution)/shard_map/cond/branch_1_fun/dot_general | solution.py:22
  13.7 1.2 %fusion = bf16[256,1024]{1,0:T(8,128)(2,1)S(1)} fusion(bf16[256,256]{1,0:T(8,128)(2,1)} %fusion.2, bf16[256,1024]{1,0:T(8,128)(2,1)S(1)} %get-tuple-element.541, bf16[256,1024]{1,0:T(8,128)(2,1)S(1)} %get-tuple-element.538), kind=kOutput, calls=%fused_computation.4 | convolution fusion | flops 135266304 | bytes 1703936 | tf_op jit(solution)/shard_map/cond/branch_1_fun/dot_general | solution.py:24
  15.0 16.9 %conditional.6 = (bf16[2,128,1024]{2,1,0:T(8,128)(2,1)S(1)}) conditional(s32[]{:T(128)} %clamp.4, bf16[2,128,1024]{2,1,0:T(8,128)(2,1)S(1)} %bitcast.118, bf16[2,128,1024]{2,1,0:T(8,128)(2,1)S(1)} %bitcast.178, bf16[2,128,1024]{2,1,0:T(8,128)(2,1)S(1)} %bitcast.61, bf16[2,128,1024]{2,1,0:T(8,128)(2,1)S(1)} %bitcast.62, ...), branch_computations={%region_5.6_spmd, %region_6.7_spmd, %region_7.8_spmd, %region_8.9_... | conditional | bytes 8 | solution.py:179
  15.0 16.8 %twin.345 = bf16[2,128,1024]{2,1,0:T(8,128)(2,1)S(1)} custom-call(bf16[2,128,1024]{2,1,0:T(8,128)(2,1)S(1)} %rows.105), custom_call_target="tpu_custom_call" | custom-call | tf_op jit(solution)/shard_map/cond/branch_105_fun/twin/pallas_call | solution.py:179
  31.8 0.0 copy-start.6
  31.8 0.0 collective-permute-done
  31.9 1.2 %broadcast_select_fusion.1 = bf16[256,1024]{1,0:T(8,128)(2,1)S(1)} fusion(bf16[256,1024]{1,0:T(8,128)(2,1)} %collective-permute-done, pred[]{:T(512)S(6)} %eq.10, bf16[1,1,256,1024]{3,2,1,0:T(8,128)(2,1)S(1)} %copy-done.3), kind=kLoop, calls=%fused_computation.45 | loop fusion | flops 262144 | bytes 1572865 | tf_op jit(solution)/shard_map/jit(_where)/select_n | solution.py:329
  33.0 0.6 collective-permute-start.1
  33.6 0.1 scatter.13
  33.7 0.1 scatter.14.masks
  33.8 0.0 copy-done.6
  33.8 0.4 conditional.7
  34.1 0.1 broadcast.124
  34.2 0.0 copy-start.4
  34.2 1.0 %copy-done.4 = f32[256,1024]{1,0:T(8,128)} copy-done((f32[256,1024]{1,0:T(8,128)}, f32[256,1024]{1,0:T(8,128)S(1)}, u32[]{:S(2)}) %copy-start.4) | copy-done | bytes 1048600
  35.2 18.3 %conditional.8 = (bf16[2,128,1024]{2,1,0:T(8,128)(2,1)S(1)}) conditional(s32[]{:T(128)} %clamp.4, bf16[2,128,1024]{2,1,0:T(8,128)(2,1)S(1)} %get-tuple-element.565, bf16[2,128,1024]{2,1,0:T(8,128)(2,1)S(1)} %get-tuple-element.565, bf16[2,128,1024]{2,1,0:T(8,128)(2,1)S(1)} %get-tuple-element.565, ...), branch_computations={%region_129.130_spmd, %region_130.131_spmd, %region_131.132_spmd, ... | conditional | bytes 8 | solution.py:179
  35.2 18.2 %twin.465 = bf16[2,128,1024]{2,1,0:T(8,128)(2,1)S(1)} custom-call(bf16[2,128,1024]{2,1,0:T(8,128)(2,1)S(1)} %rows.225), custom_call_target="tpu_custom_call" | custom-call | tf_op jit(solution)/shard_map/cond/branch_105_fun/twin/pallas_call | solution.py:179
  53.4 0.0 collective-permute-done.1
  53.4 1.1 %broadcast_select_fusion.mate_slow = bf16[256,1024]{1,0:T(8,128)(2,1)S(1)} fusion(bf16[256,1024]{1,0:T(8,128)(2,1)} %collective-permute-done.1, bf16[256,1024]{1,0:T(8,128)(2,1)S(1)} %broadcast_select_fusion.1, pred[]{:T(512)S(6)} %eq.11), kind=kLoop, calls=%fused_computation.44 | loop fusion | flops 262144 | bytes 1572865 | tf_op jit(solution)/shard_map/jit(_where)/select_n | solution.py:345
  54.5 0.0 copy-start
  54.6 0.0 copy-start.1
  54.6 0.0 copy-start.2
  54.6 2.3 %conditional.9 = (f32[256,1024]{1,0:T(8,128)}) conditional(s32[]{:T(128)} %convert_element_type.45, f32[256,1024]{1,0:T(8,128)} %copy-done.4, (bf16[2,128,1024]{2,1,0:T(8,128)(2,1)S(1)}, bf16[256,256]{1,0:T(8,128)(2,1)}) %tuple.772), branch_computations={%region_249.250_spmd, %region_250.251_spmd} | conditional | flops 134479872 | bytes 1703944 | solution.py:346
  54.6 2.3 %convolution_multiply_fusion.7 = f32[256,1024]{1,0:T(8,128)} fusion(bf16[256,256]{1,0:T(8,128)(2,1)} %get-tuple-element.547, bf16[256,1024]{1,0:T(8,128)(2,1)S(1)} %bitcast.188), kind=kOutput, calls=%fused_computation.42 | convolution fusion | flops 134479872 | bytes 1703936 | tf_op jit(solution)/shard_map/cond/branch_1_fun/dot_general | solution.py:36
  56.9 0.0 copy-done
  56.9 0.0 copy-done.1
  56.9 0.0 copy-done.2
  56.9 15.3 %outer.1 = (bf16[256,1024]{1,0:T(8,128)(2,1)S(1)}, bf16[256,1024]{1,0:T(8,128)(2,1)S(1)}) custom-call(s32[8,1024]{1,0:T(8,128)S(1)} %scatter.14.masks, f32[256,1024]{1,0:T(8,128)} %get-tuple-element.594.grad, bf16[256,1024]{1,0:T(8,128)(2,1)S(1)} %bitcast.53, bf16[256,1024]{1,0:T(8,128)(2,1)S(1)} %bitcast.54, bf16[256,1024]{1,0:T(8,128)(2,1)S(1)} %bitcast.187, ...), custom_call_target="tpu_custom_call" | custom-call | tf_op jit(solution)/shard_map/outer/pallas_call | solution.py:284
  72.2 0.8 %copy.264 = bf16[1,1,256,1024]{3,2,1,0:T(8,128)(2,1)} copy(bf16[1,1,256,1024]{3,2,1,0:T(8,128)(2,1)S(1)} %bitcast.57) | data formatting | bytes 1048576
  73.0 0.8 %copy.265 = bf16[1,1,256,1024]{3,2,1,0:T(8,128)(2,1)} copy(bf16[1,1,256,1024]{3,2,1,0:T(8,128)(2,1)S(1)} %bitcast.56) | data formatting | bytes 1048576
  (4 shorter events, 0.1 us)
Async XLA Ops:
  0.6 3.0 %copy-start.8 = (s32[2,16]{1,0:T(2,128)S(1)}, s32[2,16]{1,0:T(2,128)}, u32[]{:S(2)}) copy-start(s32[2,16]{1,0:T(2,128)} %param.266) | copy-start | bytes 388
  0.6 31.2 %collective-permute-start = (bf16[256,1024]{1,0:T(8,128)(2,1)}, bf16[256,1024]{1,0:T(8,128)(2,1)}, u32[]{:S(2)}, u32[]{:S(2)}) collective-permute-start(bf16[256,1024]{1,0:T(8,128)(2,1)} %bitcast.184), channel_id=1, source_target_pairs={{0,2},{2,0},{4,6},{6,4},{8,10},{10,8},{12,14},{14,12},{16,18},{18,... | collective-permute-start | bytes 1572872 | tf_op jit(solution)/shard_map/ppermute | solution.py:12
  6.3 0.7 copy-start.9
  9.9 1.5 %copy-start.3 = (bf16[1,1,256,1024]{3,2,1,0:T(8,128)(2,1)S(1)}, bf16[1,1,256,1024]{3,2,1,0:T(8,128)(2,1)}, u32[]{:S(2)}) copy-start(bf16[1,1,256,1024]{3,2,1,0:T(8,128)(2,1)} %param.262) | copy-start | bytes 1572868
  9.9 1.5 %copy-start.5 = (bf16[1,1,1024,256]{3,2,1,0:T(8,128)(2,1)S(1)}, bf16[1,1,1024,256]{3,2,1,0:T(8,128)(2,1)}, u32[]{:S(2)}) copy-start(bf16[1,1,1024,256]{3,2,1,0:T(8,128)(2,1)} %param.260) | copy-start | bytes 1572868
  11.7 1.0 %copy-start.7 = (bf16[1024,256]{1,0:T(8,128)(2,1)S(1)}, bf16[1024,256]{1,0:T(8,128)(2,1)}, u32[]{:S(2)}) copy-start(bf16[1024,256]{1,0:T(8,128)(2,1)} %get-tuple-element.540) | copy-start | bytes 1572868 | tf_op jit(solution)/shard_map/cond
  31.8 2.0 %copy-start.6 = (bf16[1,1,1024,256]{3,2,1,0:T(8,128)(2,1)S(1)}, bf16[1,1,1024,256]{3,2,1,0:T(8,128)(2,1)}, u32[]{:S(2)}) copy-start(bf16[1,1,1024,256]{3,2,1,0:T(8,128)(2,1)} %param.261) | copy-start | bytes 1572868
  33.0 20.4 %collective-permute-start.1 = (bf16[256,1024]{1,0:T(8,128)(2,1)S(1)}, bf16[256,1024]{1,0:T(8,128)(2,1)}, u32[]{:S(2)}, u32[]{:S(2)}) collective-permute-start(bf16[256,1024]{1,0:T(8,128)(2,1)S(1)} %broadcast_select_fusion.1), channel_id=1, source_target_pairs={{0,4},{2,6},{4,0},{6,2},{8,12},{10,14},{12,8},{14,10},{16,20},{18,... | collective-permute-start | bytes 1572872 | tf_op jit(solution)/shard_map/ppermute | solution.py:12
  34.2 1.0 %copy-start.4 = (f32[256,1024]{1,0:T(8,128)}, f32[256,1024]{1,0:T(8,128)S(1)}, u32[]{:S(2)}) copy-start(f32[256,1024]{1,0:T(8,128)S(1)} %get-tuple-element.563) | copy-start | bytes 3145732
  54.5 2.4 %copy-start = (bf16[1,1,256,1024]{3,2,1,0:T(8,128)(2,1)S(1)}, bf16[1,1,256,1024]{3,2,1,0:T(8,128)(2,1)}, u32[]{:S(2)}) copy-start(bf16[1,1,256,1024]{3,2,1,0:T(8,128)(2,1)} %param.263) | copy-start | bytes 1572868
  54.6 2.4 %copy-start.1 = (bf16[1,1,256,1024]{3,2,1,0:T(8,128)(2,1)S(1)}, bf16[1,1,256,1024]{3,2,1,0:T(8,128)(2,1)}, u32[]{:S(2)}) copy-start(bf16[1,1,256,1024]{3,2,1,0:T(8,128)(2,1)} %param.264) | copy-start | bytes 1572868
  54.6 2.4 %copy-start.2 = (bf16[1,1,256,1024]{3,2,1,0:T(8,128)(2,1)S(1)}, bf16[1,1,256,1024]{3,2,1,0:T(8,128)(2,1)}, u32[]{:S(2)}) copy-start(bf16[1,1,256,1024]{3,2,1,0:T(8,128)(2,1)} %param.265) | copy-start | bytes 1572868
